TPU v7x, 32 devices: a whole 2x2x4 slice. The times are simulated.
32 devices in a mesh: dp: 4 (over x, core), seq: 8 (over z, y).
Axes of the slice: x: 2, y: 2, z: 4, core: 2. Of those that a mesh axis runs over, the one named last changes fastest.
Arguments:
- tokens: bfloat16 [4, 1024, 768], P('dp', 'seq'), may hold values from -6 to 6
- lengths: int32 [4], P('dp'), may hold values from 256 to 1024, as said below
- qkv_weight: bfloat16 [2, 442368], P(None, ('dp', 'seq')), may hold values from -0.4375 to 0.4375
- out_weight: bfloat16 [2, 589824], P(None, ('dp', 'seq')), may hold values from -2.5 to 2.5
- up_weight: bfloat16 [2, 589824], P(None, ('dp', 'seq')), may hold values from -0.4375 to 0.4375
- down_weight: bfloat16 [2, 589824], P(None, ('dp', 'seq')), may hold values from -0.21875 to 0.21875
- norm_gain: bfloat16 [2, 1536], P(None, ('dp', 'seq')), may hold values from 0.5 to 1.5
- norm_shift: bfloat16 [2, 1536], P(None, ('dp', 'seq')), may hold values from -1.5 to 1.5
- cotangent: bfloat16 [4, 1024, 768], P('dp', 'seq'), may hold values from -6 to 6
Outputs:
- mixed: bfloat16 [4, 1024, 768], P('dp', 'seq')
- tokens_grad: bfloat16 [4, 1024, 768], P('dp', 'seq')
- qkv_grad: float32 [2, 442368], P(None, ('dp', 'seq'))
- out_grad: float32 [2, 589824], P(None, ('dp', 'seq'))
- up_grad: float32 [2, 589824], P(None, ('dp', 'seq'))
- down_grad: float32 [2, 589824], P(None, ('dp', 'seq'))
- gain_grad: float32 [2, 1536], P(None, ('dp', 'seq'))
- shift_grad: float32 [2, 1536], P(None, ('dp', 'seq'))
Inputs may be any that keep to these rules, and one draw needn't show every extreme that they name: `lengths`: valid slots of each sequence, counted from its first slot; in every draw some sequence fills all 1024 slots and some has exactly a quarter of them.
All inputs are finite; a program needn't handle non-finite values.
Results may differ from a plain program's by a relative error of at most 0.025.
Values may be sent and summed in bfloat16 or wider, within the bound.
A program may use at most 128 MiB of HBM per device.

v0:
```python
from functools import partial

import jax
import jax.numpy as jnp
from jax import lax
from jax.sharding import PartitionSpec as P

D = 768
HEADS = 12
HEAD = 64
FF = 3072
GROUPS = 4


EPSILON = 1e-06


def grouped(inputs, weight):
    count = inputs.shape[0]
    shaped = inputs.reshape(count, weight.shape[0], -1)
    result = jnp.einsum("tgi,gio->tgo", shaped, weight, preferred_element_type=jnp.float32)
    return result.reshape(count, -1)


def normalize(values, gain, shift):
    center = values - jnp.mean(values, axis=-1, keepdims=True)
    factor = lax.rsqrt(jnp.mean(center * center, axis=-1, keepdims=True) + EPSILON)
    scaled = center * factor
    return (scaled * gain + shift, scaled, factor)


def normalize_back(grad_out, scaled, factor, gain):
    weighted = grad_out * gain
    grad_in = factor * (
        weighted
        - jnp.mean(weighted, axis=-1, keepdims=True)
        - scaled * jnp.mean(weighted * scaled, axis=-1, keepdims=True)
    )
    return (grad_in, jnp.sum(grad_out * scaled, axis=0), jnp.sum(grad_out, axis=0))


def unpack(pieces):
    qkv_flat, out_flat, up_flat, down_flat, gain_flat, shift_flat = pieces
    part = D // GROUPS
    part_ff = FF // GROUPS
    return (
        qkv_flat.reshape(3, GROUPS, part, part),
        out_flat.reshape(D, D),
        up_flat.reshape(GROUPS, part, part_ff),
        down_flat.reshape(GROUPS, part_ff, part),
        gain_flat.reshape(2, D).astype(jnp.float32),
        shift_flat.reshape(2, D).astype(jnp.float32),
    )


def project_heads(rows, matrices):
    total_rows = rows.shape[0]
    part = D // GROUPS
    result = jnp.einsum(
        "tgi,cgio->ctgo",
        rows.reshape(total_rows, GROUPS, part),
        matrices,
        preferred_element_type=jnp.float32,
    ).astype(jnp.bfloat16)
    return result.reshape(matrices.shape[0], total_rows, HEADS, HEAD).transpose(0, 2, 1, 3)


def head_forward(key_ok, scaling, pieces):
    query_head, key_head, value_head = pieces
    scores = (
        jnp.einsum("td,sd->ts", query_head, key_head, preferred_element_type=jnp.float32) * scaling
    )
    scores = jnp.where(key_ok[None, :], scores, -1e30)
    largest = jnp.max(scores, axis=-1, keepdims=True)
    powers = jnp.exp(scores - largest)
    total = jnp.sum(powers, axis=-1, keepdims=True)
    probs = (powers / total).astype(jnp.bfloat16)
    result = jnp.dot(probs, value_head, preferred_element_type=jnp.float32)
    return (result, (largest + jnp.log(total))[:, 0])


def head_backward(key_ok, scaling, pieces):
    query_head, key_head, value_head, grad_head, log_total = pieces
    scores = (
        jnp.einsum("td,sd->ts", query_head, key_head, preferred_element_type=jnp.float32) * scaling
    )
    scores = jnp.where(key_ok[None, :], scores, -1e30)
    probs = jnp.exp(scores - log_total[:, None])
    grad_probs = jnp.einsum("td,sd->ts", grad_head, value_head, preferred_element_type=jnp.float32)
    delta_row = jnp.sum(probs * grad_probs, axis=-1, keepdims=True)
    grad_scores = (probs * (grad_probs - delta_row)).astype(jnp.bfloat16)
    grad_query = jnp.dot(grad_scores, key_head, preferred_element_type=jnp.float32) * scaling
    grad_key = (
        jnp.einsum("ts,td->sd", grad_scores, query_head, preferred_element_type=jnp.float32)
        * scaling
    )
    grad_value = jnp.einsum(
        "ts,td->sd", probs.astype(jnp.bfloat16), grad_head, preferred_element_type=jnp.float32
    )
    return (grad_query, grad_key, grad_value)


def per_device(
    tokens,
    lengths,
    qkv_weight,
    out_weight,
    up_weight,
    down_weight,
    norm_gain,
    norm_shift,
    cotangent,
):
    layers = qkv_weight.shape[0]
    count = tokens.shape[1]
    slots = count * lax.axis_size("seq")
    first_slot = lax.axis_index("seq") * count
    length = lengths[0]
    key_ok = jnp.arange(slots, dtype=jnp.int32) < length
    row_ok = first_slot + jnp.arange(count, dtype=jnp.int32) < length
    scaling = HEAD ** (-0.5)
    part = D // GROUPS
    part_ff = FF // GROUPS
    hidden_low = tokens[0]
    saved = []
    for layer_index in range(layers):
        gathered = (
            lax.all_gather(qkv_weight[layer_index], ("dp", "seq"), axis=0, tiled=True),
            lax.all_gather(out_weight[layer_index], ("dp", "seq"), axis=0, tiled=True),
            lax.all_gather(up_weight[layer_index], ("dp", "seq"), axis=0, tiled=True),
            lax.all_gather(down_weight[layer_index], ("dp", "seq"), axis=0, tiled=True),
            lax.all_gather(norm_gain[layer_index], ("dp", "seq"), axis=0, tiled=True),
            lax.all_gather(norm_shift[layer_index], ("dp", "seq"), axis=0, tiled=True),
        )
        project, out_matrix, up_matrix, down_matrix, gains, shifts = unpack(gathered)
        heads = project_heads(hidden_low, project)
        key_all, value_all = (
            lax.all_gather(heads[1], "seq", axis=1, tiled=True),
            lax.all_gather(heads[2], "seq", axis=1, tiled=True),
        )
        attended, log_total = lax.map(
            partial(head_forward, key_ok, scaling), (heads[0], key_all, value_all)
        )
        attended_low = attended.transpose(1, 0, 2).reshape(count, D).astype(jnp.bfloat16)
        branch = jnp.dot(attended_low, out_matrix, preferred_element_type=jnp.float32)
        middle, scaled_one, factor_one = normalize(
            hidden_low.astype(jnp.float32) + branch, gains[0], shifts[0]
        )
        middle_low = middle.astype(jnp.bfloat16)
        expanded = grouped(middle_low, up_matrix)
        activated = jax.nn.gelu(expanded, approximate=False).astype(jnp.bfloat16)
        shrunk = grouped(activated, down_matrix)
        output, scaled_two, factor_two = normalize(
            middle_low.astype(jnp.float32) + shrunk, gains[1], shifts[1]
        )
        kept = None
        saved.append(
            (
                hidden_low,
                heads,
                log_total,
                attended_low,
                middle_low,
                expanded,
                activated,
                scaled_one,
                factor_one,
                scaled_two,
                factor_two,
                kept,
            )
        )
        hidden_low = output.astype(jnp.bfloat16)
    mixed = hidden_low[None]
    grad_hidden = cotangent[0].astype(jnp.float32) * row_ok[:, None].astype(jnp.float32)
    owned_list = []
    for layer_index in reversed(range(layers)):
        (
            inputs_low,
            heads,
            log_total,
            attended_low,
            middle_low,
            expanded,
            activated,
            scaled_one,
            factor_one,
            scaled_two,
            factor_two,
            kept,
        ) = saved[layer_index]
        gathered = (
            lax.all_gather(qkv_weight[layer_index], ("dp", "seq"), axis=0, tiled=True),
            lax.all_gather(out_weight[layer_index], ("dp", "seq"), axis=0, tiled=True),
            lax.all_gather(up_weight[layer_index], ("dp", "seq"), axis=0, tiled=True),
            lax.all_gather(down_weight[layer_index], ("dp", "seq"), axis=0, tiled=True),
            lax.all_gather(norm_gain[layer_index], ("dp", "seq"), axis=0, tiled=True),
            lax.all_gather(norm_shift[layer_index], ("dp", "seq"), axis=0, tiled=True),
        )
        project, out_matrix, up_matrix, down_matrix, gains, shifts = unpack(gathered)
        key_all, value_all = (
            lax.all_gather(heads[1], "seq", axis=1, tiled=True),
            lax.all_gather(heads[2], "seq", axis=1, tiled=True),
        )
        grad_two, gain_two, shift_two = normalize_back(
            grad_hidden, scaled_two, factor_two, gains[1]
        )
        shrunk_grad = grad_two.astype(jnp.bfloat16).reshape(count, GROUPS, part)
        down_terms = jnp.einsum(
            "tgf,tgo->gfo",
            activated.reshape(count, GROUPS, part_ff),
            shrunk_grad,
            preferred_element_type=jnp.float32,
        )
        active_grad = jnp.einsum(
            "tgo,gfo->tgf", shrunk_grad, down_matrix, preferred_element_type=jnp.float32
        ).reshape(count, FF)
        unused_value, gelu_pull = jax.vjp(partial(jax.nn.gelu, approximate=False), expanded)
        expanded_grad = (
            gelu_pull(active_grad)[0].astype(jnp.bfloat16).reshape(count, GROUPS, part_ff)
        )
        up_terms = jnp.einsum(
            "tgi,tgf->gif",
            middle_low.reshape(count, GROUPS, part),
            expanded_grad,
            preferred_element_type=jnp.float32,
        )
        middle_grad = grad_two + jnp.einsum(
            "tgf,gif->tgi", expanded_grad, up_matrix, preferred_element_type=jnp.float32
        ).reshape(count, D)
        grad_one, gain_one, shift_one = normalize_back(
            middle_grad, scaled_one, factor_one, gains[0]
        )
        branch_grad = grad_one.astype(jnp.bfloat16)
        out_terms = jnp.einsum(
            "ti,to->io", attended_low, branch_grad, preferred_element_type=jnp.float32
        )
        attended_grad = jnp.einsum(
            "to,io->ti", branch_grad, out_matrix, preferred_element_type=jnp.float32
        ).astype(jnp.bfloat16)
        grad_heads = attended_grad.reshape(count, HEADS, HEAD).transpose(1, 0, 2)
        grad_query, key_terms, value_terms = lax.map(
            partial(head_backward, key_ok, scaling),
            (heads[0], key_all, value_all, grad_heads, log_total),
        )
        grad_key, grad_value = (
            lax.psum_scatter(
                key_terms.astype(jnp.bfloat16), "seq", scatter_dimension=1, tiled=True
            ).astype(jnp.float32),
            lax.psum_scatter(
                value_terms.astype(jnp.bfloat16), "seq", scatter_dimension=1, tiled=True
            ).astype(jnp.float32),
        )
        grad_projected = jnp.stack((grad_query, grad_key, grad_value)).astype(jnp.bfloat16)
        grad_projected = grad_projected.transpose(0, 2, 1, 3).reshape(3, count, GROUPS, part)
        qkv_terms = jnp.einsum(
            "tgi,ctgo->cgio",
            inputs_low.reshape(count, GROUPS, part),
            grad_projected,
            preferred_element_type=jnp.float32,
        )
        grad_hidden = grad_one + jnp.einsum(
            "ctgo,cgio->tgi", grad_projected, project, preferred_element_type=jnp.float32
        ).reshape(count, D)
        owned = (
            lax.psum_scatter(qkv_terms.reshape(-1), ("dp", "seq"), scatter_dimension=0, tiled=True),
            lax.psum_scatter(out_terms.reshape(-1), ("dp", "seq"), scatter_dimension=0, tiled=True),
            lax.psum_scatter(up_terms.reshape(-1), ("dp", "seq"), scatter_dimension=0, tiled=True),
            lax.psum_scatter(
                down_terms.reshape(-1), ("dp", "seq"), scatter_dimension=0, tiled=True
            ),
            lax.psum_scatter(
                jnp.stack((gain_one, gain_two)).reshape(-1),
                ("dp", "seq"),
                scatter_dimension=0,
                tiled=True,
            ),
            lax.psum_scatter(
                jnp.stack((shift_one, shift_two)).reshape(-1),
                ("dp", "seq"),
                scatter_dimension=0,
                tiled=True,
            ),
        )
        owned_list.insert(0, owned)
    tokens_grad = grad_hidden.astype(jnp.bfloat16)[None]
    stacked = tuple((jnp.stack([entry[member] for entry in owned_list]) for member in range(6)))
    return (
        mixed,
        tokens_grad,
        stacked[0],
        stacked[1],
        stacked[2],
        stacked[3],
        stacked[4],
        stacked[5],
    )


def solution(mesh):
    return jax.shard_map(
        per_device,
        mesh=mesh,
        in_specs=(
            P("dp", "seq", None),
            P("dp"),
            P(None, ("dp", "seq")),
            P(None, ("dp", "seq")),
            P(None, ("dp", "seq")),
            P(None, ("dp", "seq")),
            P(None, ("dp", "seq")),
            P(None, ("dp", "seq")),
            P("dp", "seq", None),
        ),
        out_specs=(
            P("dp", "seq", None),
            P("dp", "seq", None),
            P(None, ("dp", "seq")),
            P(None, ("dp", "seq")),
            P(None, ("dp", "seq")),
            P(None, ("dp", "seq")),
            P(None, ("dp", "seq")),
            P(None, ("dp", "seq")),
        ),
        check_vma=False,
    )
```

profile of v0, /device:TPU:0, one launch (start us, length us, event | category | flops | bytes accessed | tf_op | source)
XLA Modules:
  0.0 1511.1 jit_solution(13213599745147145016)
XLA Ops:
  14.8 83.9 %all-gather = bf16[1,442368]{1,0:T(2,128)(2,1)S(1)} all-gather(bf16[1,13824]{1,0:T(2,128)(2,1)S(1)} %get-tuple-element.493), channel_id=2, replica_groups=mesh['dp'=4,'seq'=8] {'dp','seq'}, dimensions={1}, use_global_device_ids=true | all-gather | bytes 912384 | tf_op jit(solution)/shard_map/all_gather | solution.py:128
  98.6 18.3 %reduce = bf16[442368]{0:T(1024)(128)(2,1)S(1)} reduce(bf16[1,442368]{1,0:T(2,128)(2,1)S(1)} %all-gather, bf16[]{:T(256)} %constant.235), dimensions={0}, to_apply=%all-gather.reduce_sub_computation | reduce | bytes 1769474 | tf_op jit(solution)/shard_map/all_gather | solution.py:128
  123.4 37.2 %all-reduce.18 = (bf16[1536]{0:T(1024)(128)(2,1)S(1)}, bf16[1536]{0:T(1024)(128)(2,1)S(1)}, bf16[1536]{0:T(1024)(128)(2,1)}, bf16[1536]{0:T(1024)(128)(2,1)}) all-reduce(bf16[1536]{0:T(1024)(128)(2,1)S(1)} %dynamic-update-slice.1, bf16[1536]{0:T(1024)(128)(2,1)S(1)} %dynamic-update-slice, ...), channel_id=7, replica_groups=mesh['dp'=4,'seq'=8] {'dp','seq'}, use_global_device_ids=true, to_apply=%add.1 | all-reduce | flops 6144 | bytes 24576
  160.6 84.0 %all-gather.8 = bf16[1,442368]{1,0:T(2,128)(2,1)S(1)} all-gather(bf16[1,13824]{1,0:T(2,128)(2,1)S(1)} %get-tuple-element.492), channel_id=10, replica_groups=mesh['dp'=4,'seq'=8] {'dp','seq'}, dimensions={1}, use_global_device_ids=true | all-gather | bytes 912384 | tf_op jit(solution)/shard_map/all_gather | solution.py:128
  244.6 18.3 %reduce.8 = bf16[442368]{0:T(1024)(128)(2,1)S(1)} reduce(bf16[1,442368]{1,0:T(2,128)(2,1)S(1)} %all-gather.8, bf16[]{:T(256)} %constant.235), dimensions={0}, to_apply=%all-gather.8.reduce_sub_computation | reduce | bytes 1769474 | tf_op jit(solution)/shard_map/all_gather | solution.py:128
  265.3 25.5 %reduce.1 = bf16[589824]{0:T(1024)(128)(2,1)S(1)} reduce(bf16[1,589824]{1,0:T(2,128)(2,1)} %all-gather.31.cloned.1.call-done, bf16[]{:T(256)} %constant.235), dimensions={0}, to_apply=%all-gather.3.reduce_sub_computation | reduce | bytes 2359298 | tf_op jit(solution)/shard_map/all_gather | solution.py:129
  290.9 1.9 reshape.329
  292.7 25.8 %reduce.4 = bf16[589824]{0:T(1024)(128)(2,1)S(1)} reduce(bf16[1,589824]{1,0:T(2,128)(2,1)} %all-gather.33.cloned.1.call-done, bf16[]{:T(256)} %constant.235), dimensions={0}, to_apply=%all-gather.6.reduce_sub_computation | reduce | bytes 2359298 | tf_op jit(solution)/shard_map/all_gather | solution.py:130
  318.5 1.9 reshape.331
  320.4 25.5 %reduce.5 = bf16[589824]{0:T(1024)(128)(2,1)S(1)} reduce(bf16[1,589824]{1,0:T(2,128)(2,1)} %all-gather.35.cloned.1.call-done, bf16[]{:T(256)} %constant.235), dimensions={0}, to_apply=%all-gather.7.reduce_sub_computation | reduce | bytes 2359298 | tf_op jit(solution)/shard_map/all_gather | solution.py:131
  345.9 1.9 reshape.332
  347.8 3.1 copy.89
  350.9 4.1 copy.90
  356.4 59.0 %while.56 = (s32[]{:T(128)}, bf16[12,128,64]{1,2,0:T(8,128)(2,1)}, f32[12,128]{1,0:T(8,128)}, bf16[12,128,64]{2,1,0:T(8,128)(2,1)S(1)}, bf16[12,1024,64]{2,1,0:T...) while((s32[]{:T(128)}, bf16[12,128,64]{1,2,0:T(8,128)(2,1)}, ...), condition=%wide.region_3.4_spmd.clone, body=%wide.region_0.3_spmd.clone.sunk | while | flops 34603904 | bytes 2172013 | solution.py:141
  391.8 1.9 fusion.271
  421.2 6.6 fusion.113
  429.2 1.9 copy.93
  435.7 2.0 fusion.139
  443.1 26.7 %reduce.9 = bf16[589824]{0:T(1024)(128)(2,1)} reduce(bf16[1,589824]{1,0:T(2,128)(2,1)} %all-gather.41.cloned.1.call-done, bf16[]{:T(256)} %constant.235), dimensions={0}, to_apply=%all-gather.11.reduce_sub_computation | reduce | bytes 2359298 | tf_op jit(solution)/shard_map/all_gather | solution.py:129
  469.8 3.3 reshape.337
  473.1 26.6 %reduce.12 = bf16[589824]{0:T(1024)(128)(2,1)} reduce(bf16[1,589824]{1,0:T(2,128)(2,1)} %all-gather.43.cloned.1.call-done, bf16[]{:T(256)} %constant.235), dimensions={0}, to_apply=%all-gather.14.reduce_sub_computation | reduce | bytes 2359298 | tf_op jit(solution)/shard_map/all_gather | solution.py:130
  499.7 3.4 reshape.339
  503.1 26.8 %reduce.13 = bf16[589824]{0:T(1024)(128)(2,1)} reduce(bf16[1,589824]{1,0:T(2,128)(2,1)} %all-gather.45.cloned.1.call-done, bf16[]{:T(256)} %constant.235), dimensions={0}, to_apply=%all-gather.15.reduce_sub_computation | reduce | bytes 2359298 | tf_op jit(solution)/shard_map/all_gather | solution.py:131
  529.8 3.6 reshape.340
  535.2 4.1 copy.98
  539.4 33.8 %all-gather.39.cloned.1.call-done = bf16[1,12,1024,64]{2,3,1,0:T(8,128)(2,1)} async-done(((bf16[1,12,128,64]{2,3,1,0:T(8,128)(2,1)}), bf16[1,12,1024,64]{2,3,1,0:T(8,128)(2,1)}) %all-gather.39.cloned.1.call-update) | async-done | bytes 1572880 | tf_op jit(solution)/shard_map/all_gather | solution.py:139
  573.2 4.1 copy.99
  578.6 70.8 %while.57 = (s32[]{:T(128)}, bf16[12,128,64]{1,2,0:T(8,128)(2,1)}, f32[12,128]{1,0:T(8,128)}, bf16[12,128,64]{2,1,0:T(8,128)(2,1)}, bf16[12,1024,64]{2,1,0:T(8,1...) while((s32[]{:T(128)}, bf16[12,128,64]{1,2,0:T(8,128)(2,1)}, ...), condition=%wide.region_11.12_spmd.clone, body=%wide.region_8.11_spmd.clone.sunk | while | flops 34603904 | bytes 2172013 | solution.py:141
  654.5 6.6 fusion.111
  662.5 1.9 copy.102
  670.6 3.4 fusion.108
  675.3 1.9 copy.105
  677.2 3.1 multiply_reduce_fusion.2
  687.6 108.3 %while.58 = (s32[]{:T(128)}, bf16[12,128,64]{1,2,0:T(8,128)(2,1)}, bf16[12,1024,64]{1,2,0:T(8,128)(2,1)}, bf16[12,1024,64]{1,2,0:T(8,128)(2,1)}, bf16[12,128,64]...) while((s32[]{:T(128)}, bf16[12,128,64]{1,2,0:T(8,128)(2,1)}, ...), condition=%wide.region_22.23_spmd.clone, body=%wide.region_20.22_spmd.clone.sunk | while | flops 85140352 | bytes 5383805 | solution.py:242
  795.9 6.1 copy.141
  802.0 6.1 reshape.420
  808.1 6.2 copy.139
  814.4 6.1 reshape.418
  820.6 50.7 %reduce-scatter.15.cloned.1.call-done = bf16[128,768]{1,0:T(8,128)(2,1)} async-done(((bf16[1024,768]{1,0:T(8,128)(2,1)}), bf16[128,768]{1,0:T(8,128)(2,1)}) %reduce-scatter.15.cloned.1.call-update) | async-done | bytes 196624
  871.2 2.1 reshape.421
  873.3 2.1 copy.142
  875.4 63.4 %reduce-scatter.13.cloned.1.call-done = bf16[128,768]{1,0:T(8,128)(2,1)} async-done(((bf16[1024,768]{1,0:T(8,128)(2,1)}), bf16[128,768]{1,0:T(8,128)(2,1)}) %reduce-scatter.13.cloned.1.call-update) | async-done | bytes 196624
  938.7 2.1 reshape.419
  940.8 2.0 copy.140
  944.8 2.5 fusion.188
  947.3 1.9 copy.111
  954.2 3.4 fusion.101
  958.9 1.9 copy.114
  960.8 2.0 multiply_reduce_fusion.4
  968.0 78.6 %while.59 = (s32[]{:T(128)}, bf16[12,128,64]{1,2,0:T(8,128)(2,1)S(1)}, bf16[12,1024,64]{1,2,0:T(8,128)(2,1)}, bf16[12,1024,64]{1,2,0:T(8,128)(2,1)}, bf16[12,128...) while((s32[]{:T(128)}, ...), condition=%wide.region_31.32_spmd.clone, body=%wide.region_29.31_spmd.clone.sunk | while | flops 85140352 | bytes 5383805 | solution.py:242
  1046.5 6.1 copy.145
  1052.7 6.1 reshape.424
  1060.2 4.8 copy.143
  1065.0 6.1 reshape.422
  1077.9 3.0 reshape.359
  1082.5 2.4 copy.124
  1084.9 3.5 reshape.353
  1095.3 3.1 reshape.358
  1098.4 24.2 %reduce-scatter.19.cloned.1.call-done = bf16[128,768]{1,0:T(8,128)(2,1)} async-done(((bf16[1024,768]{1,0:T(8,128)(2,1)}), bf16[128,768]{1,0:T(8,128)(2,1)}) %reduce-scatter.19.cloned.1.call-update) | async-done | bytes 196624
  1124.3 65.8 %reduce-scatter.17.cloned.1.call-done = bf16[128,768]{1,0:T(8,128)(2,1)} async-done(((bf16[1024,768]{1,0:T(8,128)(2,1)}), bf16[128,768]{1,0:T(8,128)(2,1)}) %reduce-scatter.17.cloned.1.call-update) | async-done | bytes 196624
  1192.3 2.1 copy.122
  1194.4 3.5 reshape.352
  1198.8 42.1 %all-reduce.16 = (f32[1536]{0:T(1024)S(1)}, f32[1536]{0:T(1024)S(1)}, f32[1536]{0:T(1024)S(1)}, f32[1536]{0:T(1024)S(1)}) all-reduce(f32[1536]{0:T(1024)S(1)} %reshape.361, f32[1536]{0:T(1024)S(1)} %reshape.360, f32[1536]{0:T(1024)S(1)} %reshape.363, f32[1536]{0:T(1024)S(1)} %reshape.362), channel_id=31, replica_groups=mesh['dp'=4,'seq'=8] {'dp','seq'}, use_global_device_ids=true, to_apply=%region_47.48.clone | all-reduce | flops 6144 | bytes 49152
  1243.7 250.3 %all-reduce.21.cloned.1.call-done = (f32[442368]{0:T(1024)}, f32[442368]{0:T(1024)}, f32[589824]{0:T(1024)}, f32[589824]{0:T(1024)}, f32[589824]{0:T(1024)}, /*i...) async-done(((f32[442368]{0:T(1024)}, f32[442368]{0:T(1024)}, f32[589824]{0:T(1024)}, f32[589824]{0:T(1024)}, f32[589824]{0:T(1024)}, /*index=5*/f32[589824]{0:T(1024)}, ...) | async-done | bytes 17694736
  (638 shorter events, 418.9 us)
Async XLA Ops:
  7.2 258.2 %all-gather.31.cloned.1.call-start = ((), (), s32[]{:S(2)}) async-start(), calls=%async_computation.6 | async-start | bytes 2433024 | tf_op jit(solution)/shard_map/all_gather | solution.py:129
  9.0 283.8 %all-gather.33.cloned.1.call-start = ((), (), s32[]{:S(2)}) async-start(), calls=%async_computation.7 | async-start | bytes 2433024 | tf_op jit(solution)/shard_map/all_gather | solution.py:130
  10.8 309.6 %all-gather.35.cloned.1.call-start = ((), (), s32[]{:S(2)}) async-start(), calls=%async_computation.8 | async-start | bytes 2433024 | tf_op jit(solution)/shard_map/all_gather | solution.py:131
  12.6 335.2 %all-gather.27.cloned.1.call-start = ((), (), s32[]{:S(2)}) async-start(), calls=%async_computation.4 | async-start | bytes 1769472 | tf_op jit(solution)/shard_map/all_gather | solution.py:138
  14.8 102.9 %copy-start.31 = (bf16[1,128,768]{1,2,0:T(8,128)(2,1)}, bf16[1,128,768]{1,2,0:T(8,128)(2,1)S(1)}, u32[]{:S(2)}) copy-start(bf16[1,128,768]{1,2,0:T(8,128)(2,1)S(1)} %copy.85) | copy-start | bytes 589828
  117.6 1.0 copy-start.17
  118.3 4.1 copy-start.56
  118.3 4.1 copy-start.57
  119.5 231.5 %all-gather.29.cloned.1.call-start = ((), (), s32[]{:S(2)}) async-start(), calls=%async_computation.5 | async-start | bytes 1769472 | tf_op jit(solution)/shard_map/all_gather | solution.py:139
  120.0 323.0 %all-gather.41.cloned.1.call-start = ((), (), s32[]{:S(2)}) async-start(), calls=%async_computation.11 | async-start | bytes 2433024 | tf_op jit(solution)/shard_map/all_gather | solution.py:129
  120.6 352.5 %all-gather.43.cloned.1.call-start = ((), (), s32[]{:S(2)}) async-start(), calls=%async_computation.12 | async-start | bytes 2433024 | tf_op jit(solution)/shard_map/all_gather | solution.py:130
  121.4 381.7 %all-gather.45.cloned.1.call-start = ((), (), s32[]{:S(2)}) async-start(), calls=%async_computation.13 | async-start | bytes 2433024 | tf_op jit(solution)/shard_map/all_gather | solution.py:131
  122.1 413.1 %all-gather.37.cloned.1.call-start = ((), (), s32[]{:S(2)}) async-start(), calls=%async_computation.9 | async-start | bytes 1769472 | tf_op jit(solution)/shard_map/all_gather | solution.py:138
  418.0 9.9 copy-start.43
  421.2 6.6 copy-start.8
  427.8 1.4 copy-start.23
  429.2 4.0 copy-start.37
  432.4 0.8 copy-start.4
  432.4 0.8 copy-start.49
  437.8 2.2 copy-start.55
  437.8 2.8 copy-start.54
  438.7 134.5 %all-gather.39.cloned.1.call-start = ((), (), s32[]{:S(2)}) async-start(), calls=%async_computation.10 | async-start | bytes 1769472 | tf_op jit(solution)/shard_map/all_gather | solution.py:139
  439.3 432.0 %reduce-scatter.15.cloned.1.call-start = ((), (), s32[]{:S(2)}) async-start(), calls=%async_computation.15 | async-start | bytes 1769472
  649.4 2.6 copy-start.36
  654.5 6.6 copy-start.9
  661.1 1.4 copy-start.24
  664.4 1.6 copy-start.28
  664.4 1.6 copy-start.52
  665.8 1.1 copy-start.6
  665.8 1.1 copy-start.50
  666.0 0.9 copy-start.53
  670.6 3.4 copy-start.16
  674.0 1.3 copy-start.19
  677.2 3.1 copy-start.1
  677.2 3.1 copy-start.45
  677.2 3.1 copy-start.48
  677.2 4.0 copy-start.3
  680.5 0.8 copy-start.10
  808.1 130.6 %reduce-scatter.13.cloned.1.call-start = ((), (), s32[]{:S(2)}) async-start(), calls=%async_computation.14 | async-start | bytes 1769472
  820.5 302.1 %reduce-scatter.19.cloned.1.call-start = ((), (), s32[]{:S(2)}) async-start(), calls=%async_computation.17 | async-start | bytes 1769472
  944.0 0.8 copy-start.14
  949.2 1.6 copy-start.5
  954.2 3.4 copy-start.15
  957.7 1.2 copy-start.21
  960.8 3.6 copy-start.2
  963.6 0.8 copy-start.12
  1046.5 6.1 copy-start.34
  1058.7 1.4 copy-start.7
  1058.8 131.3 %reduce-scatter.17.cloned.1.call-start = ((), (), s32[]{:S(2)}) async-start(), calls=%async_computation.16 | async-start | bytes 1769472
  1071.1 1.0 copy-start.11
  1071.1 1.0 copy-start.27
  1071.1 422.9 %all-reduce.21.cloned.1.call-start = ((), (), s32[]{:S(2)}) async-start(), calls=%async_computation.18 | async-start | bytes 35389440
  1072.6 1.6 copy-start.20
  1072.6 1.6 copy-start.33
  1074.6 1.6 copy-start.30
  1077.9 3.1 copy-start.29
  1084.9 3.6 copy-start.13
  1084.9 3.6 copy-start.26
  1089.0 1.6 copy-start.22
  1098.4 93.3 %copy-start.35 = (bf16[12,128,64]{1,2,0:T(8,128)(2,1)S(1)}, bf16[12,128,64]{1,2,0:T(8,128)(2,1)}, u32[]{:S(2)}) copy-start(bf16[12,128,64]{1,2,0:T(8,128)(2,1)} %copy-done.34) | copy-start | bytes 589828
  1123.9 67.9 %copy-start.32 = (bf16[1,128,768]{1,2,0:T(8,128)(2,1)S(1)}, bf16[1,128,768]{1,2,0:T(8,128)(2,1)}, u32[]{:S(2)}) copy-start(bf16[1,128,768]{1,2,0:T(8,128)(2,1)} %copy-done.31) | copy-start | bytes 589828
  1197.9 0.8 copy-start.40
  1197.9 0.8 copy-start.42
  1197.9 44.4 %copy-start.18 = (bf16[3,4,192,192]{3,2,1,0:T(8,128)(2,1)S(1)}, bf16[3,4,192,192]{3,2,1,0:T(8,128)(2,1)}, u32[]{:S(2)}) copy-start(bf16[3,4,192,192]{3,2,1,0:T(8,128)(2,1)} %copy-done.17) | copy-start | bytes 2654212
  (11 other events, 7.1 us)
Sparse Core Ops, SparseCore 0:
  11.5 63.8 all-gather.30
  78.9 59.2 all-gather.32
  141.1 59.4 all-gather.34
  203.1 53.2 all-gather.26
  258.9 44.1 all-gather.28
  306.4 55.4 all-gather.40
  365.5 56.3 all-gather.42
  424.8 56.0 all-gather.44
  483.0 44.1 all-gather.36
  529.7 43.4 all-gather.38
  808.2 62.9 reduce-scatter.14
  874.9 63.7 reduce-scatter.12
  1058.9 63.7 reduce-scatter.18
  1126.3 63.7 reduce-scatter.16
  1198.1 295.8 all-reduce.20
where the time goes:
time: 1530 us; the launch traced here: 1510 us
  waiting for transfers between devices  491 us (32%)
  other arithmetic  269 us (18%)
  matrix products  260 us (17%)
  blocking collectives  247 us (16%)
  local copies, waits for them, and re-layouts  226 us (15%)
  between operations  15.8 us (1%)
    unnamed x20, waiting for transfers between devices  457 us
    all_gather x2, blocking collectives, per_device(): lax.all_gather(qkv_weight[layer_index], ('dp', 'seq'), axis=0, tiled=True)  168 us
    unnamed x161, local copies, waits for them, and re-layouts  94.9 us
    unnamed x2, blocking collectives  79.3 us
    all_gather x2, other arithmetic, per_device(): lax.all_gather(up_weight[layer_index], ('dp', 'seq'), axis=0, tiled=True)  52.3 us
    all_gather x2, other arithmetic, per_device(): lax.all_gather(down_weight[layer_index], ('dp', 'seq'), axis=0, tiled=True)  52.3 us
    all_gather x2, other arithmetic, per_device(): lax.all_gather(out_weight[layer_index], ('dp', 'seq'), axis=0, tiled=True)  52.3 us
    dot_general x24, matrix products, head_forward(): result = jnp.dot(probs, value_head, preferred_element_type=jnp.float32)  44.6 us
  transfers between devices with their start and end apart: 15, of which 6 were waited for; matrix products, arithmetic and copies ran while one was open for 25% of the time, Pallas kernels for 0%

commit v1 on v0

--- a/solution.py
+++ b/solution.py
@@ -1,8 +1,11 @@
+import types
 from functools import partial
 
 import jax
 import jax.numpy as jnp
 from jax import lax
+from jax.experimental import pallas as pl
+from jax.experimental.pallas import tpu as pltpu
 from jax.sharding import PartitionSpec as P
 
 D = 768
@@ -297,9 +300,640 @@
     )
 
 
+F32 = jnp.float32
+BF16 = jnp.bfloat16
+PART = D // GROUPS
+PART_FF = FF // GROUPS
+LAYERS = 2
+ROWS = 128
+HALF = 4 * ROWS
+FULL = 2 * HALF
+NDEV = 32
+UNIT = PART // 8
+HEADS_HERE = HEADS // GROUPS
+KEY_BLOCK = 256
+FF_BLOCK = 128
+SEMS = 512
+MESH = pl.DeviceIdType.MESH
+
+SCRATCH = dict(
+    x_all=((LAYERS, PART, FULL), BF16),
+    cot_t=((PART, HALF), BF16),
+    tok_t=((D, ROWS), BF16),
+    cotown_t=((D, ROWS), BF16),
+    ln_in=((8, 128), F32),
+    gn_in=((2, PART, 128), BF16),
+    wq_in=((LAYERS, 8, 3, UNIT, PART), BF16),
+    wr_in=((LAYERS, 8, GROUPS, UNIT, PART), BF16),
+    wc_in=((LAYERS, 8, GROUPS, UNIT, PART), BF16),
+    wu_in=((LAYERS, 8, UNIT, PART_FF), BF16),
+    wd_in=((LAYERS, 8, PART_FF // 8, PART), BF16),
+    wn_q=((LAYERS, 3, PART, PART), BF16),
+    wn_r=((LAYERS, GROUPS, PART, PART), BF16),
+    wn_u=((LAYERS, PART, PART_FF), BF16),
+    wn_d=((LAYERS, PART_FF, PART), BF16),
+    wt_u=((PART_FF, PART), BF16),
+    bias=((FULL, 128), F32),
+    q_t=((LAYERS, PART, HALF), BF16),
+    k_t=((LAYERS, PART, FULL), BF16),
+    v_t=((LAYERS, PART, FULL), BF16),
+    k_n=((LAYERS, HEADS_HERE, FULL, HEAD), BF16),
+    v_n=((LAYERS, HEADS_HERE, FULL, HEAD), BF16),
+    p_t=((LAYERS, HEADS_HERE, FULL, HALF), BF16),
+    rinv=((LAYERS, HEADS_HERE, 8, HALF), F32),
+    s_scr=((FULL, HALF), F32),
+    ds_scr=((FULL, HALF), BF16),
+    o_t=((LAYERS, PART, HALF), F32),
+    att_all=((LAYERS, D, HALF), BF16),
+    bg_all=((LAYERS, D, HALF), BF16),
+    xh1=((LAYERS, PART, HALF), F32),
+    xh2=((LAYERS, PART, HALF), F32),
+    r1=((LAYERS, 8, HALF), F32),
+    r2=((LAYERS, 8, HALF), F32),
+    mid=((LAYERS, PART, HALF), BF16),
+    act=((LAYERS, PART_FF, HALF), BF16),
+    dgl=((LAYERS, PART_FF, HALF), F32),
+    eg=((LAYERS, PART_FF, HALF), BF16),
+    sgb=((LAYERS, PART, HALF), BF16),
+    fg=((PART, HALF), F32),
+    do_t=((PART, HALF), BF16),
+    dq_t=((PART, HALF), BF16),
+    dk_t=((PART, FULL), BF16),
+    dv_t=((PART, FULL), BF16),
+    dx_out=((LAYERS, PART, HALF), F32),
+    dx_in=((LAYERS, PART, HALF), F32),
+    stats=((4 * LAYERS, 4, 8, HALF), F32),
+    mix_out=((PART, HALF), BF16),
+    mix_in=((D, ROWS), BF16),
+    tg_out=((PART, HALF), BF16),
+    tg_in=((D, ROWS), BF16),
+    gs_acc=((2, PART, 128), F32),
+    gs_in=((8, PART // 4, 128), F32),
+    gb_d=((LAYERS, 8, PART_FF // 8, PART), BF16),
+    gb_u=((LAYERS, 8, UNIT, PART_FF), BF16),
+    gb_o=((LAYERS, 8, GROUPS, UNIT, PART), BF16),
+    gb_q=((LAYERS, 8, 3, UNIT, PART), BF16),
+    sb_d=((LAYERS, 4, PART_FF // 8, PART), BF16),
+    sb_u=((LAYERS, 4, UNIT, PART_FF), BF16),
+    sb_o=((LAYERS, 4, GROUPS, UNIT, PART), BF16),
+    sb_q=((LAYERS, 4, 3, UNIT, PART), BF16),
+    gm_d=((LAYERS, 4, PART_FF // 8, PART), BF16),
+    gm_u=((LAYERS, 4, UNIT, PART_FF), BF16),
+    gm_o=((LAYERS, 4, GROUPS, UNIT, PART), BF16),
+    gm_q=((LAYERS, 4, 3, UNIT, PART), BF16),
+    rg_d=((LAYERS, 4, PART_FF // 8, PART), BF16),
+    rg_u=((LAYERS, 4, UNIT, PART_FF), BF16),
+    rg_o=((LAYERS, 4, GROUPS, UNIT, PART), BF16),
+    rg_q=((LAYERS, 4, 3, UNIT, PART), BF16),
+)
+
+
+def mm(a, b):
+    return jnp.dot(a, b, preferred_element_type=F32)
+
+
+def mm_nt(a, b):
+    return lax.dot_general(a, b, (((1,), (1,)), ((), ())), preferred_element_type=F32)
+
+
+def rows_of(units):
+    count, rows, columns = units.shape
+    return units.astype(F32).reshape(count * rows, columns).astype(BF16)
+
+
+def units_of(matrix):
+    rows, columns = matrix.shape
+    return matrix.reshape(rows // UNIT, UNIT, columns).astype(BF16)
+
+
+def erf_pair(v):
+    cdf = 0.5 * (1.0 + lax.erf(v * (0.5**0.5)))
+    slope = cdf + v * (jnp.exp(-0.5 * v * v) * 0.3989422804014327)
+    return cdf, slope
+
+
+def fast_kernel(
+    tokens, cotangent, length, misc, w_qkv, w_out, w_up, w_down,
+    mixed, tokens_grad, g_qkv, g_out, g_up, g_down, g_norm,
+    sems, *scratch,
+):
+    b = types.SimpleNamespace(**dict(zip(SCRATCH, scratch)))
+    p, s = lax.axis_index("dp"), lax.axis_index("seq")
+    x, c, z, y = p // 2, p % 2, s // 2, s % 2
+    g = 2 * x + y
+    own = pl.multiple_of(HALF * c, HALF)
+    other = pl.multiple_of(HALF * (1 - c), HALF)
+    g_rows = pl.multiple_of(PART * g, PART)
+    used = [0]
+    pending = []
+
+    def new_sems(count=1):
+        first = used[0]
+        used[0] += count
+        assert used[0] <= SEMS
+        return first
+
+    def dev(dx, dc, dz, dy):
+        return (2 * dx + dc, 2 * dz + dy)
+
+    sibling = dev(x, 1 - c, z, y)
+    square = (dev(x, c, z, 1 - y), dev(1 - x, c, z, y), dev(1 - x, c, z, 1 - y))
+
+    def send(src, dst, to, arrive, maybe_here=False):
+        copy = pltpu.make_async_remote_copy(
+            src, dst, sems.at[new_sems()], sems.at[arrive], device_id=to, device_id_type=MESH
+        )
+        if not maybe_here:
+            copy.start()
+            pending.append((copy, None))
+            return
+        away = jnp.logical_or(to[0] != p, to[1] != s)
+
+        @pl.when(away)
+        def _():
+            copy.start()
+
+        @pl.when(jnp.logical_not(away))
+        def _():
+            pltpu.make_async_copy(src, dst, sems.at[arrive]).start()
+
+        pending.append((copy, away))
+
+    def arrived(ref, arrive):
+        pltpu.make_async_copy(ref, ref, sems.at[arrive]).wait()
+
+    me = 8 * p + s
+    barrier = pltpu.get_barrier_semaphore()
+
+    def greet(i, carry):
+        d = (me + i) % NDEV
+        pl.semaphore_signal(barrier, inc=1, device_id=(d // 8, d % 8), device_id_type=MESH)
+        return carry
+
+    lax.fori_loop(1, NDEV, greet, 0)
+    b.tok_t[...] = tokens[...].T
+    b.cotown_t[...] = cotangent[...].T
+    b.gs_acc[...] = jnp.zeros((2, PART, 128), F32)
+    pl.semaphore_wait(barrier, NDEV - 1)
+
+    tok_sem, len_sem, cot_sem, gn_sem = (new_sems() for _ in range(4))
+    half_of = s // 4
+    for gg in range(4):
+        to = dev(gg // 2, half_of, p, gg % 2)
+        lane = pl.multiple_of(ROWS * s, ROWS)
+        send(
+            b.tok_t.at[pl.ds(PART * gg, PART), :],
+            b.x_all.at[0, :, pl.ds(lane, ROWS)],
+            to, tok_sem, True,
+        )
+    len_copies = []
+    first_chunk = s % 4 == 0
+    for gg in range(4):
+        to = dev(gg // 2, half_of, p, gg % 2)
+        away = jnp.logical_or(to[0] != p, to[1] != s)
+        copy = pltpu.make_async_remote_copy(
+            length, b.ln_in, sems.at[new_sems()], sems.at[len_sem], device_id=to, device_id_type=MESH
+        )
+
+        @pl.when(jnp.logical_and(first_chunk, away))
+        def _():
+            copy.start()
+
+        @pl.when(jnp.logical_and(first_chunk, jnp.logical_not(away)))
+        def _():
+            pltpu.make_async_copy(length, b.ln_in, sems.at[len_sem]).start()
+
+        pending.append((copy, jnp.logical_and(first_chunk, away)))
+
+    weights_in = dict(q=b.wq_in, r=b.wr_in, c=b.wc_in, u=b.wu_in, d=b.wd_in)
+    arrive_w = {(name, l): new_sems() for l in range(LAYERS) for name in "qrcud"}
+    relay_w = {(name, l): new_sems() for l in range(LAYERS) for name in "qrcud"}
+
+    def send_qkv(l):
+        for k in range(3):
+            u = 3 * me + k
+            cc, gg, t = u // 32, (u % 32) // 8, u % 8
+            for zz in range(4):
+                send(
+                    w_qkv.at[l, k], b.wq_in.at[l, t, cc],
+                    dev(gg // 2, t // 4, zz, gg % 2), arrive_w["q", l], True,
+                )
+
+    def send_out(l):
+        for zz in range(4):
+            send(w_out.at[l], b.wr_in.at[l, s], dev(p // 2, s // 4, zz, p % 2), arrive_w["r", l], True)
+        for cg in range(4):
+            for zz in range(4):
+                send(
+                    w_out.at[l, cg], b.wc_in.at[l, s, p],
+                    dev(cg // 2, s // 4, zz, cg % 2), arrive_w["c", l], True,
+                )
+
+    def send_updown(l):
+        for zz in range(4):
+            send(w_up.at[l], b.wu_in.at[l, s], dev(p // 2, s // 4, zz, p % 2), arrive_w["u", l], True)
+        for zz in range(4):
+            send(w_down.at[l], b.wd_in.at[l, s], dev(p // 2, s // 4, zz, p % 2), arrive_w["d", l], True)
+
+    def relay(name, l):
+        buffer = weights_in[name]
+        mine = buffer.at[l, pl.ds(4 * c, 4)]
+        arrived(mine, arrive_w[name, l])
+        send(mine, mine, sibling, relay_w[name, l])
+
+    def relayed(name, l):
+        arrived(weights_in[name].at[l, pl.ds(4 * (1 - c), 4)], relay_w[name, l])
+
+    send_qkv(0)
+    for zz in range(4):
+        for cc in range(2):
+            gg = 2 * (p % 2) + s // 4
+            row = pl.multiple_of(48 * (s % 4), 16)
+            send(
+                misc, b.gn_in.at[p // 2, pl.ds(row, 48), :],
+                dev(gg // 2, cc, zz, gg % 2), gn_sem, True,
+            )
+    send_out(0)
+    send_updown(0)
+    for gg in range(4):
+        lane = pl.multiple_of(ROWS * (s % 4), ROWS)
+        send(
+            b.cotown_t.at[pl.ds(PART * gg, PART), :], b.cot_t.at[:, pl.ds(lane, ROWS)],
+            dev(gg // 2, half_of, p, gg % 2), cot_sem, True,
+        )
+    send_qkv(1)
+    send_out(1)
+    send_updown(1)
+
+    x_sem = [new_sems() for _ in range(LAYERS)]
+    x_half = b.x_all.at[0, :, pl.ds(own, HALF)]
+    arrived(x_half, tok_sem)
+    send(x_half, x_half, sibling, x_sem[0])
+    relay("q", 0)
+    arrived(b.ln_in, len_sem)
+    valid = b.ln_in[0:1, 0:1]
+    key_at = lax.broadcasted_iota(jnp.int32, (FULL, 128), 0).astype(F32)
+    b.bias[...] = jnp.where(key_at < valid, 0.0, -1e30)
+    arrived(b.gn_in, gn_sem)
+
+    def gain_shift(l, k):
+        columns = b.gn_in[k].astype(F32)
+        return columns[:, 2 * l : 2 * l + 1], columns[:, 2 * l + 1 : 2 * l + 2]
+
+    stat_used = [0]
+
+    def exchange(first, second):
+        i = stat_used[0]
+        stat_used[0] += 1
+        buffer = b.stats.at[i]
+        buffer[0] = jnp.concatenate([first, second, jnp.zeros((6, HALF), F32)], axis=0)
+        base = new_sems(3)
+        for d in range(3):
+            send(buffer.at[0], buffer.at[d + 1], square[d], base + d)
+
+        def finish():
+            for d in range(3):
+                arrived(buffer.at[d + 1], base + d)
+            return [(buffer[d, 0:1], buffer[d, 1:2]) for d in range(4)]
+
+        return finish
+
+    def normalize_here(v, name, l, gain, shift):
+        mean_here = jnp.sum(v, axis=0, keepdims=True) * (1.0 / PART)
+        d = v - mean_here
+        finish = exchange(mean_here, jnp.sum(d * d, axis=0, keepdims=True))
+        pairs = finish()
+        mean = (pairs[0][0] + pairs[1][0] + pairs[2][0] + pairs[3][0]) * 0.25
+        total = sum(m2 + PART * (m1 - mean) * (m1 - mean) for m1, m2 in pairs)
+        factor = lax.rsqrt(total * (1.0 / D) + EPSILON)
+        scaled = (v - mean) * factor
+        getattr(b, "xh" + name)[l] = scaled
+        getattr(b, "r" + name)[l, 0:1] = factor
+        return scaled * gain + shift
+
+    att_sem = [[new_sems(3) for _ in range(3)] for _ in range(LAYERS)]
+    att_send = [[new_sems(3) for _ in range(3)] for _ in range(LAYERS)]
+
+    def forward(l):
+        x_own = b.x_all[l, :, pl.ds(own, HALF)]
+        if l > 0:
+            relay("q", l)
+        relayed("q", l)
+        turned = []
+        for cc in range(3):
+            nat = rows_of(b.wq_in[l, :, cc])
+            b.wn_q[l, cc] = nat
+            turned.append(nat.T)
+        b.q_t[l] = mm(turned[0], x_own).astype(BF16) * jnp.asarray(0.125, BF16)
+
+        def keys_values(start, part):
+            for matrix, name in ((turned[1], "k"), (turned[2], "v")):
+                value = mm(matrix, part).astype(BF16)
+                getattr(b, name + "_t")[l, :, pl.ds(start, HALF)] = value
+                for h in range(HEADS_HERE):
+                    getattr(b, name + "_n")[l, h, pl.ds(start, HALF), :] = value[HEAD * h : HEAD * (h + 1)].T
+
+        keys_values(own, x_own)
+        arrived(b.x_all.at[l, :, pl.ds(other, HALF)], x_sem[l])
+        keys_values(other, b.x_all[l, :, pl.ds(other, HALF)])
+
+        def one_head(h, carry):
+            head = pl.multiple_of(HEAD * h, HEAD)
+            q = b.q_t[l, pl.ds(head, HEAD), :]
+            largest = jnp.full((1, HALF), -jnp.inf, F32)
+            for kb in range(0, FULL, KEY_BLOCK):
+                scores = mm(b.k_n[l, h, kb : kb + KEY_BLOCK, :], q) + b.bias[kb : kb + KEY_BLOCK, 0:1]
+                b.s_scr[kb : kb + KEY_BLOCK] = scores
+                largest = jnp.maximum(largest, jnp.max(scores, axis=0, keepdims=True))
+            total = jnp.zeros((1, HALF), F32)
+            for kb in range(0, FULL, KEY_BLOCK):
+                powers = jnp.exp(b.s_scr[kb : kb + KEY_BLOCK] - largest)
+                total += jnp.sum(powers, axis=0, keepdims=True)
+                b.p_t[l, h, kb : kb + KEY_BLOCK] = powers.astype(BF16)
+            inverse = 1.0 / total
+            b.rinv[l, h, 0:1] = inverse
+            out = mm(b.v_t[l, pl.ds(head, HEAD), :], b.p_t[l, h]) * inverse
+            b.o_t[l, pl.ds(head, HEAD), :] = out
+            rows = pl.ds(pl.multiple_of(g_rows + head, HEAD), HEAD)
+            b.att_all[l, rows, :] = out.astype(BF16)
+            piece = b.att_all.at[l, rows, :]
+            for d in range(3):
+                pltpu.make_async_remote_copy(
+                    piece, piece, sems.at[att_send[l][d] + h], sems.at[att_sem[l][d] + h],
+                    device_id=square[d], device_id_type=MESH,
+                ).start()
+            return carry
+
+        lax.fori_loop(0, HEADS_HERE, one_head, 0)
+        for name in "cudr":
+            relay(name, l)
+        relayed("c", l)
+        turned = [rows_of(b.wc_in[l, :, r]).T for r in range(4)]
+        relayed("u", l)
+        nat = rows_of(b.wu_in[l])
+        b.wn_u[l] = nat
+        b.wt_u[...] = nat.T
+        relayed("d", l)
+        nat = b.wd_in[l].reshape(PART_FF, PART)
+        b.wn_d[l] = nat
+        down_t = nat.T
+        flips = ((0, 1), (1, 0), (1, 1))
+        for h in range(HEADS_HERE):
+            for d, (fx, fy) in enumerate(flips):
+                px = 1 - x if fx else x
+                py = 1 - y if fy else y
+                start = pl.multiple_of(PART * (2 * px + py) + HEAD * h, HEAD)
+                arrived(b.att_all.at[l, pl.ds(start, HEAD), :], att_sem[l][d] + h)
+        branch = sum(mm(turned[r], b.att_all[l, PART * r : PART * (r + 1), :]) for r in range(4))
+        gain, shift = gain_shift(l, 0)
+        middle = normalize_here(x_own.astype(F32) + branch, "1", l, gain, shift).astype(BF16)
+        b.mid[l] = middle
+
+        def one_block(i, carry):
+            rows = pl.ds(pl.multiple_of(FF_BLOCK * i, FF_BLOCK), FF_BLOCK)
+            expanded = mm(b.wt_u[rows, :], b.mid[l])
+            cdf, slope = erf_pair(expanded)
+            b.act[l, rows, :] = (expanded * cdf).astype(BF16)
+            b.dgl[l, rows, :] = slope
+            return carry
+
+        lax.fori_loop(0, PART_FF // FF_BLOCK, one_block, 0)
+        second = middle.astype(F32) + mm(down_t, b.act[l])
+        gain, shift = gain_shift(l, 1)
+        return normalize_here(second, "2", l, gain, shift)
+
+    hidden = forward(0)
+    b.x_all[1, :, pl.ds(own, HALF)] = hidden.astype(BF16)
+    x_half = b.x_all.at[1, :, pl.ds(own, HALF)]
+    send(x_half, x_half, sibling, x_sem[1])
+    hidden = forward(1)
+
+    mix_sem, tg_sem = new_sems(), new_sems()
+
+    def send_back(value, out_ref, in_ref, arrive):
+        out_ref[...] = value.astype(BF16)
+        for k in range(4):
+            send(
+                out_ref.at[:, ROWS * k : ROWS * (k + 1)], in_ref.at[pl.ds(g_rows, PART), :],
+                (z, 4 * c + k), arrive, True,
+            )
+
+    send_back(hidden, b.mix_out, b.mix_in, mix_sem)
+
+    half_sem = {(name, l): new_sems() for l in range(LAYERS) for name in "duoq"}
+    owner_sem = {(name, l): new_sems() for l in range(LAYERS) for name in "duoq"}
+
+    def to_sibling(name, l):
+        send(
+            getattr(b, "gb_" + name).at[l, pl.ds(4 * (1 - c), 4)], getattr(b, "sb_" + name).at[l], sibling, half_sem[name, l]
+        )
+
+    def to_owners(name, l):
+        arrived(getattr(b, "sb_" + name).at[l], half_sem[name, l])
+        mine = getattr(b, "gb_" + name)[l, pl.ds(4 * c, 4)].astype(F32) + getattr(b, "sb_" + name)[l].astype(F32)
+        getattr(b, "gm_" + name)[l] = mine.astype(BF16)
+        for k in range(4):
+            t = 4 * c + k
+            if name != "q":
+                send(getattr(b, "gm_" + name).at[l, k], getattr(b, "rg_" + name).at[l, z], (g, t), owner_sem[name, l], True)
+                continue
+            for cc in range(3):
+                u = 32 * cc + 8 * g + t
+                j = u // 3
+                send(
+                    b.gm_q.at[l, k, cc], b.rg_q.at[l, z, u % 3], (j // 8, j % 8), owner_sem["q", l], True
+                )
+
+    lane_at = lax.broadcasted_iota(jnp.int32, (PART, 128), 1)
+
+    def normalize_back_here(grad, name, l, k):
+        gain, _ = gain_shift(l, k)
+        scaled = getattr(b, "xh" + name)[l]
+        weighted = grad * gain
+        finish = exchange(
+            jnp.sum(weighted, axis=0, keepdims=True), jnp.sum(weighted * scaled, axis=0, keepdims=True)
+        )
+        gain_grad = jnp.sum(grad * scaled, axis=1, keepdims=True)
+        shift_grad = jnp.sum(grad, axis=1, keepdims=True)
+        b.gs_acc[k] += jnp.where(lane_at == 2 * l, gain_grad, 0.0) + jnp.where(
+            lane_at == 2 * l + 1, shift_grad, 0.0
+        )
+        pairs = finish()
+        one = (pairs[0][0] + pairs[1][0] + pairs[2][0] + pairs[3][0]) * (1.0 / D)
+        two = (pairs[0][1] + pairs[1][1] + pairs[2][1] + pairs[3][1]) * (1.0 / D)
+        return getattr(b, "r" + name)[l, 0:1] * (weighted - one - scaled * two)
+
+    bg_sem = [new_sems(3) for _ in range(LAYERS)]
+    dx_sem = [new_sems() for _ in range(LAYERS)]
+
+    def backward(l, grad):
+        second_grad = normalize_back_here(grad, "2", l, 1)
+        b.sgb[l] = second_grad.astype(BF16)
+        if l + 1 < LAYERS:
+            to_owners("q", l + 1)
+
+        def one_block(i, carry):
+            rows = pl.ds(pl.multiple_of(FF_BLOCK * i, FF_BLOCK), FF_BLOCK)
+            active_grad = mm(b.wn_d[l, rows, :], b.sgb[l])
+            b.eg[l, rows, :] = (active_grad * b.dgl[l, rows, :]).astype(BF16)
+            return carry
+
+        lax.fori_loop(0, PART_FF // FF_BLOCK, one_block, 0)
+        middle_grad = second_grad + mm(b.wn_u[l], b.eg[l])
+        first_grad = normalize_back_here(middle_grad, "1", l, 0)
+        b.fg[...] = first_grad
+        b.bg_all[l, pl.ds(g_rows, PART), :] = first_grad.astype(BF16)
+        piece = b.bg_all.at[l, pl.ds(g_rows, PART), :]
+        for d in range(3):
+            send(piece, piece, square[d], bg_sem[l] + d)
+        grads = mm_nt(b.act[l], b.sgb[l])
+        b.gb_d[l] = grads.astype(BF16).reshape(8, PART_FF // 8, PART)
+        to_sibling("d", l)
+        b.gb_u[l] = units_of(mm_nt(b.mid[l], b.eg[l]))
+        to_sibling("u", l)
+        relayed("r", l)
+        for cg in range(4):
+            b.wn_r[l, cg] = rows_of(b.wr_in[l, :, cg])
+        for d, (fx, fy) in enumerate(((0, 1), (1, 0), (1, 1))):
+            px = 1 - x if fx else x
+            py = 1 - y if fy else y
+            start = pl.multiple_of(PART * (2 * px + py), PART)
+            arrived(b.bg_all.at[l, pl.ds(start, PART), :], bg_sem[l] + d)
+        attended_grad = sum(mm(b.wn_r[l, r], b.bg_all[l, PART * r : PART * (r + 1), :]) for r in range(4))
+        b.do_t[...] = attended_grad.astype(BF16)
+        att = b.att_all[l, pl.ds(g_rows, PART), :]
+        for cg in range(4):
+            b.gb_o[l, :, cg] = units_of(mm_nt(att, b.bg_all[l, PART * cg : PART * (cg + 1), :]))
+        to_sibling("o", l)
+
+        def one_head(h, carry):
+            head = pl.multiple_of(HEAD * h, HEAD)
+            rows = pl.ds(head, HEAD)
+            inverse = b.rinv[l, h, 0:1]
+            grad_out = b.do_t[rows, :].astype(F32)
+            delta = jnp.sum(grad_out * b.o_t[l, rows, :], axis=0, keepdims=True) * inverse
+            grad_scaled = (grad_out * inverse).astype(BF16)
+            for kb in range(0, FULL, KEY_BLOCK):
+                block = slice(kb, kb + KEY_BLOCK)
+                grad_probs = mm(b.v_n[l, h, block, :], grad_scaled)
+                b.ds_scr[block] = (b.p_t[l, h, block].astype(F32) * (grad_probs - delta)).astype(BF16)
+            b.dq_t[rows, :] = (mm(b.k_t[l, rows, :], b.ds_scr[...]) * 0.125).astype(BF16)
+            b.dk_t[rows, :] = mm_nt(b.q_t[l, rows, :], b.ds_scr[...]).astype(BF16)
+            b.dv_t[rows, :] = mm_nt(grad_scaled, b.p_t[l, h]).astype(BF16)
+            return carry
+
+        lax.fori_loop(0, HEADS_HERE, one_head, 0)
+        w_q, w_k, w_v = (b.wn_q[l, cc] for cc in range(3))
+        b.dx_out[l] = mm(w_k, b.dk_t[:, pl.ds(other, HALF)]) + mm(w_v, b.dv_t[:, pl.ds(other, HALF)])
+        send(b.dx_out.at[l], b.dx_in.at[l], sibling, dx_sem[l])
+        x_own = b.x_all[l, :, pl.ds(own, HALF)]
+        b.gb_q[l, :, 0] = units_of(mm_nt(x_own, b.dq_t[...]))
+        b.gb_q[l, :, 1] = units_of(mm_nt(b.x_all[l], b.dk_t[...]))
+        b.gb_q[l, :, 2] = units_of(mm_nt(b.x_all[l], b.dv_t[...]))
+        to_sibling("q", l)
+        for name in "duo":
+            to_owners(name, l)
+        here = mm(w_q, b.dq_t[...])
+        here += mm(w_k, b.dk_t[:, pl.ds(own, HALF)]) + mm(w_v, b.dv_t[:, pl.ds(own, HALF)])
+        arrived(b.dx_in.at[l], dx_sem[l])
+        return b.fg[...] + here + b.dx_in[l]
+
+    arrived(b.cot_t, cot_sem)
+    position = lax.broadcasted_iota(jnp.int32, (PART, HALF), 1) + HALF * c
+    grad = jnp.where(position.astype(F32) < valid, b.cot_t[...].astype(F32), 0.0)
+    grad = backward(1, grad)
+    grad = backward(0, grad)
+    send_back(grad, b.tg_out, b.tg_in, tg_sem)
+    to_owners("q", 0)
+
+    gs_sem = new_sems()
+    for k in range(2):
+        for q in range(4):
+            send(
+                b.gs_acc.at[k, 48 * q : 48 * (q + 1), :], b.gs_in.at[2 * z + c],
+                (2 * k + g // 2, 4 * (g % 2) + q), gs_sem, True,
+            )
+
+    arrived(b.mix_in, mix_sem)
+    mixed[...] = b.mix_in[...].T
+    for l in reversed(range(LAYERS)):
+        for name, out in (("d", g_down), ("u", g_up), ("o", g_out), ("q", g_qkv)):
+            arrived(getattr(b, "rg_" + name).at[l], owner_sem[name, l])
+            out[l] = sum(getattr(b, "rg_" + name)[l, i].astype(F32) for i in range(4))
+    arrived(b.tg_in, tg_sem)
+    tokens_grad[...] = b.tg_in[...].T
+    arrived(b.gs_in, gs_sem)
+    g_norm[...] = sum(b.gs_in[i] for i in range(8))
+
+    for copy, when in pending:
+        if when is None:
+            copy.wait_send()
+        else:
+            pl.when(when)(copy.wait_send)
+    for l in range(LAYERS):
+        for h in range(HEADS_HERE):
+            for d in range(3):
+                piece = b.att_all.at[l, pl.ds(pl.multiple_of(g_rows + HEAD * h, HEAD), HEAD), :]
+                pltpu.make_async_remote_copy(
+                    piece, piece, sems.at[att_send[l][d] + h], sems.at[att_sem[l][d] + h],
+                    device_id=square[d], device_id_type=MESH,
+                ).wait_send()
+
+
+def fast_device(
+    tokens, lengths, qkv_weight, out_weight, up_weight, down_weight, norm_gain, norm_shift, cotangent
+):
+    length = jnp.full((8, 128), lengths[0], F32)
+    misc = jnp.stack([norm_gain[0], norm_shift[0], norm_gain[1], norm_shift[1]], axis=1)
+    misc = jnp.pad(misc, ((0, 0), (0, 124)))
+    operands = (
+        tokens[0],
+        cotangent[0],
+        length,
+        misc,
+        qkv_weight.reshape(LAYERS, 3, UNIT, PART),
+        out_weight.reshape(LAYERS, UNIT, GROUPS, PART).transpose(0, 2, 1, 3),
+        up_weight.reshape(LAYERS, UNIT, PART_FF),
+        down_weight.reshape(LAYERS, PART_FF // 8, PART),
+    )
+    vmem = pl.BlockSpec(memory_space=pltpu.VMEM)
+    shapes = (
+        ((ROWS, D), BF16),
+        ((ROWS, D), BF16),
+        ((LAYERS, 3, UNIT, PART), F32),
+        ((LAYERS, GROUPS, UNIT, PART), F32),
+        ((LAYERS, UNIT, PART_FF), F32),
+        ((LAYERS, PART_FF // 8, PART), F32),
+        ((PART // 4, 128), F32),
+    )
+    mixed, tokens_grad, g_qkv, g_out, g_up, g_down, g_norm = pl.pallas_call(
+        fast_kernel,
+        out_shape=tuple(jax.ShapeDtypeStruct(*shape) for shape in shapes),
+        in_specs=[vmem] * len(operands),
+        out_specs=tuple([vmem] * len(shapes)),
+        scratch_shapes=[pltpu.SemaphoreType.DMA((SEMS,))] + [pltpu.VMEM(*entry) for entry in SCRATCH.values()],
+        compiler_params=pltpu.CompilerParams(
+            collective_id=0, has_side_effects=True, vmem_limit_bytes=60 * 2**20
+        ),
+        name="encoder",
+    )(*operands)
+    g_norm = g_norm[:, :4].T
+    return (
+        mixed[None],
+        tokens_grad[None],
+        g_qkv.reshape(LAYERS, -1),
+        g_out.transpose(0, 2, 1, 3).reshape(LAYERS, -1),
+        g_up.reshape(LAYERS, -1),
+        g_down.reshape(LAYERS, -1),
+        g_norm[0::2],
+        g_norm[1::2],
+    )
+
+
 def solution(mesh):
+    small = (mesh.shape["dp"], mesh.shape["seq"]) == (4, 8)
     return jax.shard_map(
-        per_device,
+        fast_device if small else per_device,
         mesh=mesh,
         in_specs=(
             P("dp", "seq", None),

time: 1530 us -> 182 us (0.12); the launches traced: 1510 us -> 182 us
  waiting for transfers between devices: 491 us -> 0 us
  other arithmetic: 269 us -> 0.01 us
  matrix products: 260 us -> 0 us
  blocking collectives: 247 us -> 0 us
  local copies, waits for them, and re-layouts: 226 us -> 12.9 us
  Pallas kernels: 0 us -> 168 us
    unnamed x20 -> x0, waiting for transfers between devices: 457 us -> none
    dot_general x192 -> x0, matrix products: 260 us -> none  [the longest x24 44.6 us: head_forward(): result = jnp.dot(probs, value_head, preferred_element_type=jnp.float32)]
    all_gather x8 -> x0, other arithmetic: 194 us -> none  [the longest x2 52.3 us: per_device(): lax.all_gather(up_weight[layer_index], ('dp', 'seq'), axis=0, tiled=True)]
    all_gather x2 -> x0, blocking collectives: 168 us -> none  [per_device(): lax.all_gather(qkv_weight[layer_index], ('dp', 'seq'), axis=0, tiled=True)]
    pallas_call x0 -> x1, Pallas kernels: none -> 168 us  [fast_device(): pl.pallas_call(fast_kernel, out_shape=tuple((jax.ShapeDtypeStruct(*shape)...]
    unnamed x161 -> x26, local copies, waits for them, and re-layouts: 94.9 us -> 5.05 us
    unnamed x2 -> x0, blocking collectives: 79.3 us -> none
    reshape x26 -> x7, local copies, waits for them, and re-layouts: 47.5 us -> 4.79 us  [the longest x1 0.9 us: fast_device(): g_out.transpose(0, 2, 1, 3).reshape(LAYERS, -1)]
  transfers between devices with their start and end apart: 15 -> 0, of which waited for: 6 -> 0; matrix products, arithmetic and copies ran while one was open for 25% -> 0% of each run, Pallas kernels for 0% -> 0%
where the time goes in v1:
time: 182 us
  Pallas kernels  168 us (92%)
  local copies, waits for them, and re-layouts  12.9 us (7%)
    pallas_call x1, Pallas kernels, fast_device(): pl.pallas_call(fast_kernel, out_shape=tuple((jax.ShapeDtypeStruct(*shape)...  168 us
    unnamed x26, local copies, waits for them, and re-layouts  5.05 us

profile of v1, /device:TPU:0, one launch (start us, length us, event | category | flops | bytes accessed | tf_op | source)
XLA Modules:
  0.0 182.0 jit_solution(15837602176407385814)
XLA Ops:
  0.6 0.0 copy-start.9
  1.3 0.7 slice_bitcast_fusion.3
  2.1 0.6 broadcast_in_dim.9.length
  2.6 0.1 copy.31
  2.8 0.0 copy-start.6
  2.8 0.6 pad.4.misc
  3.4 0.0 copy-done.9
  3.4 0.7 reshape.41.w_qkv
  4.1 0.0 copy-done.6
  4.1 0.0 copy-start.7
  4.1 0.6 copy.41
  4.8 0.3 copy-done.7
  5.0 0.1 reshape.42
  5.1 0.0 copy-start.8
  5.2 0.7 copy.40
  5.8 0.2 copy-done.8
  6.0 0.8 reshape.44.w_down
  6.8 167.8 %encoder.1 = (bf16[128,768]{1,0:T(8,128)(2,1)}, bf16[128,768]{1,0:T(8,128)(2,1)}, f32[2,3,24,192]{3,2,1,0:T(8,128)}, f32[2,4,24,192]{3,2,1,0:T(8,128)}, f32[2,24...) custom-call(bf16[128,768]{1,0:T(8,128)(2,1)} %bitcast.32, bf16[128,768]{1,0:T(8,128)(2,1)} %bitcast.33, ...), custom_call_target="tpu_custom_call" | custom-call | tf_op jit(solution)/shard_map/encoder/pallas_call | solution.py:909
  174.6 0.0 copy-start.5
  174.6 0.8 slice_bitcast_fusion
  175.4 0.1 slice.27
  175.4 0.6 copy.35
  176.1 0.1 slice.26
  176.2 0.0 copy-start.4
  176.2 0.6 copy.34
  176.8 0.0 copy-done.5
  176.8 0.8 reshape.45
  177.6 0.0 copy-done.4
  177.6 0.0 copy-start.3
  177.6 0.7 copy.37
  178.3 0.0 copy-start.2
  178.3 0.2 copy-done.3
  178.5 0.8 reshape.48
  179.4 0.0 copy-done.2
  179.4 0.1 copy.33
  179.4 0.0 copy-start.1
  179.4 0.9 reshape.46
  180.3 0.0 copy-done.1
  180.4 0.0 copy-start
  180.4 0.7 copy.45
  181.0 0.3 copy-done
  181.4 0.7 copy.46
  (1 shorter events, 0.0 us)
Async XLA Ops:
  0.6 2.7 %copy-start.9 = (bf16[2,13824]{1,0:T(2,128)(2,1)S(1)}, bf16[2,13824]{1,0:T(2,128)(2,1)}, u32[]{:S(2)}) copy-start(bf16[2,13824]{1,0:T(2,128)(2,1)} %param.11) | copy-start | bytes 165892
  2.8 1.4 copy-start.6
  4.1 0.9 copy-start.7
  5.1 0.9 copy-start.8
  174.6 2.2 %copy-start.5 = (f32[2,3,24,192]{3,2,1,0:T(8,128)S(1)}, f32[2,3,24,192]{3,2,1,0:T(8,128)}, u32[]{:S(2)}) copy-start(f32[2,3,24,192]{3,2,1,0:T(8,128)} %get-tuple-element.17) | copy-start | bytes 331780
  176.2 1.4 copy-start.4
  177.6 0.9 copy-start.3
  178.3 1.0 copy-start.2
  179.4 0.9 copy-start.1
  180.4 1.0 copy-start

commit v2 on v1

--- a/solution.py
+++ b/solution.py
@@ -310,6 +310,7 @@
 FULL = 2 * HALF
 NDEV = 32
 UNIT = PART // 8
+FLAT = UNIT * PART_FF // 128
 HEADS_HERE = HEADS // GROUPS
 KEY_BLOCK = 256
 FF_BLOCK = 128
@@ -323,13 +324,21 @@
     cotown_t=((D, ROWS), BF16),
     ln_in=((8, 128), F32),
     gn_in=((2, PART, 128), BF16),
-    wq_in=((LAYERS, 8, 3, UNIT, PART), BF16),
-    wr_in=((LAYERS, 8, GROUPS, UNIT, PART), BF16),
-    wc_in=((LAYERS, 8, GROUPS, UNIT, PART), BF16),
-    wu_in=((LAYERS, 8, UNIT, PART_FF), BF16),
-    wd_in=((LAYERS, 8, PART_FF // 8, PART), BF16),
+    misc=((128, 128), BF16),
+    ln_out=((8, 128), F32),
+    wq_out=((LAYERS, 3, 2 * UNIT, 128), BF16),
+    wc_out=((LAYERS, GROUPS, 2 * UNIT, 128), BF16),
+    wr_out=((LAYERS, FLAT, 128), BF16),
+    wm_out=((LAYERS, 2, FLAT, 128), BF16),
+    wq_in=((LAYERS, 3, 8, 2 * UNIT, 128), BF16),
+    wc_in=((LAYERS, GROUPS, 8, 2 * UNIT, 128), BF16),
+    wr_in=((LAYERS, 8, FLAT, 128), BF16),
+    wm_in=((LAYERS, 8, 2, FLAT, 128), BF16),
+    raw=((8 * FLAT, 128), F32),
+    left=((PART_FF, 128), F32),
+    right=((PART_FF, 128), F32),
     wn_q=((LAYERS, 3, PART, PART), BF16),
-    wn_r=((LAYERS, GROUPS, PART, PART), BF16),
+    wn_r=((LAYERS, PART, D), BF16),
     wn_u=((LAYERS, PART, PART_FF), BF16),
     wn_d=((LAYERS, PART_FF, PART), BF16),
     wt_u=((PART_FF, PART), BF16),
@@ -368,23 +377,24 @@
     tg_out=((PART, HALF), BF16),
     tg_in=((D, ROWS), BF16),
     gs_acc=((2, PART, 128), F32),
-    gs_in=((8, PART // 4, 128), F32),
-    gb_d=((LAYERS, 8, PART_FF // 8, PART), BF16),
-    gb_u=((LAYERS, 8, UNIT, PART_FF), BF16),
-    gb_o=((LAYERS, 8, GROUPS, UNIT, PART), BF16),
-    gb_q=((LAYERS, 8, 3, UNIT, PART), BF16),
-    sb_d=((LAYERS, 4, PART_FF // 8, PART), BF16),
-    sb_u=((LAYERS, 4, UNIT, PART_FF), BF16),
-    sb_o=((LAYERS, 4, GROUPS, UNIT, PART), BF16),
-    sb_q=((LAYERS, 4, 3, UNIT, PART), BF16),
-    gm_d=((LAYERS, 4, PART_FF // 8, PART), BF16),
-    gm_u=((LAYERS, 4, UNIT, PART_FF), BF16),
-    gm_o=((LAYERS, 4, GROUPS, UNIT, PART), BF16),
-    gm_q=((LAYERS, 4, 3, UNIT, PART), BF16),
-    rg_d=((LAYERS, 4, PART_FF // 8, PART), BF16),
-    rg_u=((LAYERS, 4, UNIT, PART_FF), BF16),
-    rg_o=((LAYERS, 4, GROUPS, UNIT, PART), BF16),
-    rg_q=((LAYERS, 4, 3, UNIT, PART), BF16),
+    gs_out=((2, 4, 8, 128), F32),
+    gs_in=((8, 8, 128), F32),
+    gb_d=((LAYERS, 8, FLAT, 128), BF16),
+    gb_u=((LAYERS, 8, FLAT, 128), BF16),
+    gb_o=((LAYERS, 8, FLAT, 128), BF16),
+    gb_q=((LAYERS, 8, 3, 2 * UNIT, 128), BF16),
+    sb_d=((LAYERS, 4, FLAT, 128), BF16),
+    sb_u=((LAYERS, 4, FLAT, 128), BF16),
+    sb_o=((LAYERS, 4, FLAT, 128), BF16),
+    sb_q=((LAYERS, 4, 3, 2 * UNIT, 128), BF16),
+    gm_d=((LAYERS, 4, FLAT, 128), BF16),
+    gm_u=((LAYERS, 4, FLAT, 128), BF16),
+    gm_o=((LAYERS, 4, FLAT, 128), BF16),
+    gm_q=((LAYERS, 4, 3, 2 * UNIT, 128), BF16),
+    rg_d=((LAYERS, 4, FLAT, 128), BF16),
+    rg_u=((LAYERS, 4, FLAT, 128), BF16),
+    rg_o=((LAYERS, 4, FLAT, 128), BF16),
+    rg_q=((LAYERS, 4, 3, 2 * UNIT, 128), BF16),
 )
 
 
@@ -396,14 +406,48 @@
     return lax.dot_general(a, b, (((1,), (1,)), ((), ())), preferred_element_type=F32)
 
 
-def rows_of(units):
-    count, rows, columns = units.shape
-    return units.astype(F32).reshape(count * rows, columns).astype(BF16)
+def turn(v):
+    return pltpu.roll(v, 64, axis=1)
+
+
+def low_lanes(a, b):
+    return jnp.where(lax.broadcasted_iota(jnp.int32, a.shape, 1) < 64, a, b)
+
+
+def every(start, count, step):
+    return pl.ds(start, count, stride=step)
+
+
+def rows_from_triples(first, second, third, left, right):
+    count = first.shape[0]
+    second_turned, third_turned = turn(second), turn(third)
+    left[every(0, count, 2), :] = first
+    left[every(1, count, 2), :] = low_lanes(second_turned, third_turned)
+    right[every(0, count, 2), :] = second
+    right[every(1, count, 2), :] = third_turned
+
+
+def triples_from_rows(count, left, right):
+    turned = turn(left[every(1, count, 2), :])
+    first = left[every(0, count, 2), :]
+    second = low_lanes(right[every(0, count, 2), :], turned)
+    third = low_lanes(turned, turn(right[every(1, count, 2), :]))
+    return first, second, third
+
+
+def matrix_of(units):
+    count = units.shape[0]
+    wide = units.astype(F32)
+    left = wide[:, :UNIT].reshape(UNIT * count, 128)
+    right = wide[:, UNIT:].reshape(UNIT * count, 128)
+    return jnp.concatenate([left, right[:, :64]], axis=1).astype(BF16)
 
 
 def units_of(matrix):
-    rows, columns = matrix.shape
-    return matrix.reshape(rows // UNIT, UNIT, columns).astype(BF16)
+    count = matrix.shape[0] // UNIT
+    left = matrix[:, :128].reshape(count, UNIT, 128)
+    right = jnp.concatenate([matrix[:, 128:], matrix[:, :64]], axis=1).reshape(count, UNIT, 128)
+    return jnp.concatenate([left, right], axis=1).astype(BF16)
 
 
 def erf_pair(v):
@@ -413,7 +457,7 @@
 
 
 def fast_kernel(
-    tokens, cotangent, length, misc, w_qkv, w_out, w_up, w_down,
+    tokens, cotangent, length, gains, shifts, w_qkv, w_out, w_up, w_down,
     mixed, tokens_grad, g_qkv, g_out, g_up, g_down, g_norm,
     sems, *scratch,
 ):
@@ -421,6 +465,8 @@
     p, s = lax.axis_index("dp"), lax.axis_index("seq")
     x, c, z, y = p // 2, p % 2, s // 2, s % 2
     g = 2 * x + y
+    seq_here = jnp.where(z == 3, 3, (z + 2) % 3)
+    z_mine = jnp.where(p == 3, 3, (p + 1) % 3)
     own = pl.multiple_of(HALF * c, HALF)
     other = pl.multiple_of(HALF * (1 - c), HALF)
     g_rows = pl.multiple_of(PART * g, PART)
@@ -474,12 +520,24 @@
     b.tok_t[...] = tokens[...].T
     b.cotown_t[...] = cotangent[...].T
     b.gs_acc[...] = jnp.zeros((2, PART, 128), F32)
+    b.ln_out[...] = jnp.full((8, 128), length[0].astype(F32), F32)
+    norm_rows = [ref[...].astype(F32)[l : l + 1] for l in range(LAYERS) for ref in (gains, shifts)]
+    norm_rows = jnp.concatenate(norm_rows + [jnp.zeros((4, 48), F32)], axis=0)
+    norm_rows = jnp.concatenate([norm_rows, jnp.zeros((8, 80), F32)], axis=1)
+    norm_rows = jnp.concatenate([norm_rows, jnp.zeros((120, 128), F32)], axis=0)
+    b.misc[...] = norm_rows.T.astype(BF16)
+    b.raw[0:216] = w_qkv[...].astype(F32)
+    for l in range(LAYERS):
+        rows_from_triples(*(b.raw[every(l + 2 * i, 36, 6), :] for i in range(3)), b.left, b.right)
+        for k in range(3):
+            rows = slice(UNIT * k, UNIT * (k + 1))
+            b.wq_out[l, k] = jnp.concatenate([b.left[rows], b.right[rows]], axis=0).astype(BF16)
     pl.semaphore_wait(barrier, NDEV - 1)
 
     tok_sem, len_sem, cot_sem, gn_sem = (new_sems() for _ in range(4))
     half_of = s // 4
     for gg in range(4):
-        to = dev(gg // 2, half_of, p, gg % 2)
+        to = dev(gg // 2, half_of, z_mine, gg % 2)
         lane = pl.multiple_of(ROWS * s, ROWS)
         send(
             b.tok_t.at[pl.ds(PART * gg, PART), :],
@@ -489,10 +547,10 @@
     len_copies = []
     first_chunk = s % 4 == 0
     for gg in range(4):
-        to = dev(gg // 2, half_of, p, gg % 2)
+        to = dev(gg // 2, half_of, z_mine, gg % 2)
         away = jnp.logical_or(to[0] != p, to[1] != s)
         copy = pltpu.make_async_remote_copy(
-            length, b.ln_in, sems.at[new_sems()], sems.at[len_sem], device_id=to, device_id_type=MESH
+            b.ln_out, b.ln_in, sems.at[new_sems()], sems.at[len_sem], device_id=to, device_id_type=MESH
         )
 
         @pl.when(jnp.logical_and(first_chunk, away))
@@ -501,13 +559,13 @@
 
         @pl.when(jnp.logical_and(first_chunk, jnp.logical_not(away)))
         def _():
-            pltpu.make_async_copy(length, b.ln_in, sems.at[len_sem]).start()
+            pltpu.make_async_copy(b.ln_out, b.ln_in, sems.at[len_sem]).start()
 
         pending.append((copy, jnp.logical_and(first_chunk, away)))
 
-    weights_in = dict(q=b.wq_in, r=b.wr_in, c=b.wc_in, u=b.wu_in, d=b.wd_in)
-    arrive_w = {(name, l): new_sems() for l in range(LAYERS) for name in "qrcud"}
-    relay_w = {(name, l): new_sems() for l in range(LAYERS) for name in "qrcud"}
+    weights_in = dict(q=b.wq_in, r=b.wr_in, c=b.wc_in, m=b.wm_in)
+    arrive_w = {(name, l): new_sems() for l in range(LAYERS) for name in "qrcm"}
+    relay_w = {(name, l): new_sems() for l in range(LAYERS) for name in "qrcm"}
 
     def send_qkv(l):
         for k in range(3):
@@ -515,34 +573,38 @@
             cc, gg, t = u // 32, (u % 32) // 8, u % 8
             for zz in range(4):
                 send(
-                    w_qkv.at[l, k], b.wq_in.at[l, t, cc],
+                    b.wq_out.at[l, k], b.wq_in.at[l, cc, t],
                     dev(gg // 2, t // 4, zz, gg % 2), arrive_w["q", l], True,
                 )
 
-    def send_out(l):
-        for zz in range(4):
-            send(w_out.at[l], b.wr_in.at[l, s], dev(p // 2, s // 4, zz, p % 2), arrive_w["r", l], True)
+    def send_columns(l):
         for cg in range(4):
             for zz in range(4):
                 send(
-                    w_out.at[l, cg], b.wc_in.at[l, s, p],
+                    b.wc_out.at[l, cg], b.wc_in.at[l, p, s],
                     dev(cg // 2, s // 4, zz, cg % 2), arrive_w["c", l], True,
                 )
 
+    def send_rows(l):
+        for zz in range(4):
+            send(b.wr_out.at[l], b.wr_in.at[l, s], dev(p // 2, s // 4, zz, p % 2), arrive_w["r", l], True)
+
     def send_updown(l):
         for zz in range(4):
-            send(w_up.at[l], b.wu_in.at[l, s], dev(p // 2, s // 4, zz, p % 2), arrive_w["u", l], True)
-        for zz in range(4):
-            send(w_down.at[l], b.wd_in.at[l, s], dev(p // 2, s // 4, zz, p % 2), arrive_w["d", l], True)
+            send(b.wm_out.at[l], b.wm_in.at[l, s], dev(p // 2, s // 4, zz, p % 2), arrive_w["m", l], True)
+
+    def half(name, l, which):
+        ref = weights_in[name]
+        units = pl.ds(4 * which, 4)
+        return ref.at[l, :, units] if name in "qc" else ref.at[l, units]
 
     def relay(name, l):
-        buffer = weights_in[name]
-        mine = buffer.at[l, pl.ds(4 * c, 4)]
+        mine = half(name, l, c)
         arrived(mine, arrive_w[name, l])
         send(mine, mine, sibling, relay_w[name, l])
 
     def relayed(name, l):
-        arrived(weights_in[name].at[l, pl.ds(4 * (1 - c), 4)], relay_w[name, l])
+        arrived(half(name, l, 1 - c), relay_w[name, l])
 
     send_qkv(0)
     for zz in range(4):
@@ -550,26 +612,34 @@
             gg = 2 * (p % 2) + s // 4
             row = pl.multiple_of(48 * (s % 4), 16)
             send(
-                misc, b.gn_in.at[p // 2, pl.ds(row, 48), :],
+                b.misc.at[0:48, :], b.gn_in.at[p // 2, pl.ds(row, 48), :],
                 dev(gg // 2, cc, zz, gg % 2), gn_sem, True,
             )
-    send_out(0)
-    send_updown(0)
-    for gg in range(4):
-        lane = pl.multiple_of(ROWS * (s % 4), ROWS)
-        send(
-            b.cotown_t.at[pl.ds(PART * gg, PART), :], b.cot_t.at[:, pl.ds(lane, ROWS)],
-            dev(gg // 2, half_of, p, gg % 2), cot_sem, True,
-        )
-    send_qkv(1)
-    send_out(1)
-    send_updown(1)
+    b.raw[0:288] = w_out[...].astype(F32)
+    for l in range(LAYERS):
+        b.wr_out[l] = b.raw[every(l, FLAT, 2), :].astype(BF16)
+        parts = [b.raw[every(2 * i + l, UNIT, 12), :] for i in range(6)]
+        turned = [turn(part) for part in parts]
+        pieces = (
+            (parts[0], parts[1]),
+            (low_lanes(turned[1], turned[2]), turned[2]),
+            (parts[3], parts[4]),
+            (low_lanes(turned[4], turned[5]), turned[5]),
+        )
+        for cg in range(4):
+            b.wc_out[l, cg] = jnp.concatenate(pieces[cg], axis=0).astype(BF16)
+    for i, ref in enumerate((w_up, w_down)):
+        b.raw[0:288] = ref[...].astype(F32)
+        for l in range(LAYERS):
+            b.wm_out[l, i] = b.raw[every(l, FLAT, 2), :].astype(BF16)
 
     x_sem = [new_sems() for _ in range(LAYERS)]
     x_half = b.x_all.at[0, :, pl.ds(own, HALF)]
     arrived(x_half, tok_sem)
     send(x_half, x_half, sibling, x_sem[0])
     relay("q", 0)
+    send_columns(0)
+    send_updown(0)
     arrived(b.ln_in, len_sem)
     valid = b.ln_in[0:1, 0:1]
     key_at = lax.broadcasted_iota(jnp.int32, (FULL, 128), 0).astype(F32)
@@ -582,11 +652,11 @@
 
     stat_used = [0]
 
-    def exchange(first, second):
+    def exchange(*rows):
         i = stat_used[0]
         stat_used[0] += 1
         buffer = b.stats.at[i]
-        buffer[0] = jnp.concatenate([first, second, jnp.zeros((6, HALF), F32)], axis=0)
+        buffer[0] = jnp.concatenate([*rows, jnp.zeros((8 - len(rows), HALF), F32)], axis=0)
         base = new_sems(3)
         for d in range(3):
             send(buffer.at[0], buffer.at[d + 1], square[d], base + d)
@@ -594,34 +664,60 @@
         def finish():
             for d in range(3):
                 arrived(buffer.at[d + 1], base + d)
-            return [(buffer[d, 0:1], buffer[d, 1:2]) for d in range(4)]
+            return [[buffer[d, i : i + 1] for i in range(len(rows))] for d in range(4)]
 
         return finish
 
-    def normalize_here(v, name, l, gain, shift):
+    def normalize_here(v, name, l, gain, shift, weighted=None):
         mean_here = jnp.sum(v, axis=0, keepdims=True) * (1.0 / PART)
         d = v - mean_here
-        finish = exchange(mean_here, jnp.sum(d * d, axis=0, keepdims=True))
-        pairs = finish()
-        mean = (pairs[0][0] + pairs[1][0] + pairs[2][0] + pairs[3][0]) * 0.25
-        total = sum(m2 + PART * (m1 - mean) * (m1 - mean) for m1, m2 in pairs)
+        rows = [mean_here, jnp.sum(d * d, axis=0, keepdims=True)]
+        if weighted is not None:
+            rows += [jnp.sum(weighted, axis=0, keepdims=True), jnp.sum(weighted * d, axis=0, keepdims=True)]
+        exchanged = exchange(*rows)
+        return lambda: normalize_there(exchanged(), v, name, l, gain, shift, weighted)
+
+    def normalize_there(four, v, name, l, gain, shift, weighted):
+        mean = (four[0][0] + four[1][0] + four[2][0] + four[3][0]) * 0.25
+        total = sum(f[1] + PART * (f[0] - mean) * (f[0] - mean) for f in four)
         factor = lax.rsqrt(total * (1.0 / D) + EPSILON)
         scaled = (v - mean) * factor
         getattr(b, "xh" + name)[l] = scaled
         getattr(b, "r" + name)[l, 0:1] = factor
-        return scaled * gain + shift
+        result = scaled * gain + shift
+        if weighted is None:
+            return result
+        one = sum(f[2] for f in four) * (1.0 / D)
+        two = sum(f[3] + (f[0] - mean) * f[2] for f in four) * factor * (1.0 / D)
+        return result, one, two
+
+    def wide_rows(units, into):
+        b.raw[...] = units.astype(F32).reshape(8 * FLAT, 128)
+        for i in range(6):
+            into[:, 128 * i : 128 * (i + 1)] = b.raw[every(i, PART, 6), :].astype(BF16)
+
+    def flat_units(matrix):
+        for i in range(6):
+            b.raw[every(i, PART, 6), :] = matrix[:, 128 * i : 128 * (i + 1)]
+        return b.raw[...].astype(BF16).reshape(8, FLAT, 128)
 
     att_sem = [[new_sems(3) for _ in range(3)] for _ in range(LAYERS)]
     att_send = [[new_sems(3) for _ in range(3)] for _ in range(LAYERS)]
 
+    def send_cotangent():
+        for gg in range(4):
+            lane = pl.multiple_of(ROWS * (s % 4), ROWS)
+            send(
+                b.cotown_t.at[pl.ds(PART * gg, PART), :], b.cot_t.at[:, pl.ds(lane, ROWS)],
+                dev(gg // 2, half_of, z_mine, gg % 2), cot_sem, True,
+            )
+
     def forward(l):
         x_own = b.x_all[l, :, pl.ds(own, HALF)]
-        if l > 0:
-            relay("q", l)
         relayed("q", l)
         turned = []
         for cc in range(3):
-            nat = rows_of(b.wq_in[l, :, cc])
+            nat = matrix_of(b.wq_in[l, cc])
             b.wn_q[l, cc] = nat
             turned.append(nat.T)
         b.q_t[l] = mm(turned[0], x_own).astype(BF16) * jnp.asarray(0.125, BF16)
@@ -665,18 +761,9 @@
             return carry
 
         lax.fori_loop(0, HEADS_HERE, one_head, 0)
-        for name in "cudr":
-            relay(name, l)
+        relay("c", l)
         relayed("c", l)
-        turned = [rows_of(b.wc_in[l, :, r]).T for r in range(4)]
-        relayed("u", l)
-        nat = rows_of(b.wu_in[l])
-        b.wn_u[l] = nat
-        b.wt_u[...] = nat.T
-        relayed("d", l)
-        nat = b.wd_in[l].reshape(PART_FF, PART)
-        b.wn_d[l] = nat
-        down_t = nat.T
+        columns_t = matrix_of(b.wc_in[l].reshape(32, 2 * UNIT, 128)).T
         flips = ((0, 1), (1, 0), (1, 1))
         for h in range(HEADS_HERE):
             for d, (fx, fy) in enumerate(flips):
@@ -684,9 +771,22 @@
                 py = 1 - y if fy else y
                 start = pl.multiple_of(PART * (2 * px + py) + HEAD * h, HEAD)
                 arrived(b.att_all.at[l, pl.ds(start, HEAD), :], att_sem[l][d] + h)
-        branch = sum(mm(turned[r], b.att_all[l, PART * r : PART * (r + 1), :]) for r in range(4))
+        relay("m", l)
+        branch = mm(columns_t, b.att_all[l])
         gain, shift = gain_shift(l, 0)
-        middle = normalize_here(x_own.astype(F32) + branch, "1", l, gain, shift).astype(BF16)
+        finish = normalize_here(x_own.astype(F32) + branch, "1", l, gain, shift)
+        relayed("m", l)
+        wide_rows(b.wm_in[l, :, 0], b.wn_u.at[l])
+        b.wt_u[...] = b.wn_u[l].T
+        b.raw[...] = b.wm_in[l, :, 1].astype(F32).reshape(8 * FLAT, 128)
+        rows_from_triples(*(b.raw[every(i, PART_FF // 2, 3), :] for i in range(3)), b.left, b.right)
+        nat = jnp.concatenate([b.left[...], b.right[:, 0:64]], axis=1).astype(BF16)
+        b.wn_d[l] = nat
+        down_t = nat.T
+        middle = finish().astype(BF16)
+        if l == 0:
+            send_qkv(1)
+            send_cotangent()
         b.mid[l] = middle
 
         def one_block(i, carry):
@@ -700,13 +800,23 @@
         lax.fori_loop(0, PART_FF // FF_BLOCK, one_block, 0)
         second = middle.astype(F32) + mm(down_t, b.act[l])
         gain, shift = gain_shift(l, 1)
-        return normalize_here(second, "2", l, gain, shift)
+        if l + 1 < LAYERS:
+            return normalize_here(second, "2", l, gain, shift)()
+        arrived(b.cot_t, cot_sem)
+        position = lax.broadcasted_iota(jnp.int32, (PART, HALF), 1) + HALF * c
+        grad = jnp.where(position.astype(F32) < valid, b.cot_t[...].astype(F32), 0.0)
+        return normalize_here(second, "2", l, gain, shift, grad * gain)(), grad
 
     hidden = forward(0)
     b.x_all[1, :, pl.ds(own, HALF)] = hidden.astype(BF16)
     x_half = b.x_all.at[1, :, pl.ds(own, HALF)]
     send(x_half, x_half, sibling, x_sem[1])
-    hidden = forward(1)
+    relay("q", 1)
+    send_columns(1)
+    send_updown(1)
+    send_rows(1)
+    send_rows(0)
+    (hidden, one, two), grad = forward(1)
 
     mix_sem, tg_sem = new_sems(), new_sems()
 
@@ -715,7 +825,7 @@
         for k in range(4):
             send(
                 out_ref.at[:, ROWS * k : ROWS * (k + 1)], in_ref.at[pl.ds(g_rows, PART), :],
-                (z, 4 * c + k), arrive, True,
+                (seq_here, 4 * c + k), arrive, True,
             )
 
     send_back(hidden, b.mix_out, b.mix_in, mix_sem)
@@ -746,28 +856,45 @@
 
     lane_at = lax.broadcasted_iota(jnp.int32, (PART, 128), 1)
 
-    def normalize_back_here(grad, name, l, k):
-        gain, _ = gain_shift(l, k)
-        scaled = getattr(b, "xh" + name)[l]
-        weighted = grad * gain
-        finish = exchange(
-            jnp.sum(weighted, axis=0, keepdims=True), jnp.sum(weighted * scaled, axis=0, keepdims=True)
-        )
+    def norm_grads(grad, scaled, l, k):
         gain_grad = jnp.sum(grad * scaled, axis=1, keepdims=True)
         shift_grad = jnp.sum(grad, axis=1, keepdims=True)
         b.gs_acc[k] += jnp.where(lane_at == 2 * l, gain_grad, 0.0) + jnp.where(
             lane_at == 2 * l + 1, shift_grad, 0.0
         )
-        pairs = finish()
-        one = (pairs[0][0] + pairs[1][0] + pairs[2][0] + pairs[3][0]) * (1.0 / D)
-        two = (pairs[0][1] + pairs[1][1] + pairs[2][1] + pairs[3][1]) * (1.0 / D)
+
+    def normalize_back_here(grad, name, l, k, known=None):
+        gain, _ = gain_shift(l, k)
+        scaled = getattr(b, "xh" + name)[l]
+        weighted = grad * gain
+        if known is None:
+            finish = exchange(
+                jnp.sum(weighted, axis=0, keepdims=True), jnp.sum(weighted * scaled, axis=0, keepdims=True)
+            )
+            norm_grads(grad, scaled, l, k)
+            four = finish()
+            one, two = (sum(f[i] for f in four) * (1.0 / D) for i in range(2))
+        else:
+            one, two = known
         return getattr(b, "r" + name)[l, 0:1] * (weighted - one - scaled * two)
+
+    gs_sem = new_sems()
+
+    def send_norm_grads():
+        for k in range(2):
+            turned = b.gs_acc[k].T[0:8]
+            for q in range(4):
+                b.gs_out[k, q] = jnp.concatenate([turned[:, 48 * q : 48 * (q + 1)], jnp.zeros((8, 80), F32)], axis=1)
+                send(
+                    b.gs_out.at[k, q], b.gs_in.at[2 * z + c], (2 * k + g // 2, 4 * (g % 2) + q), gs_sem, True
+                )
 
     bg_sem = [new_sems(3) for _ in range(LAYERS)]
     dx_sem = [new_sems() for _ in range(LAYERS)]
 
-    def backward(l, grad):
-        second_grad = normalize_back_here(grad, "2", l, 1)
+    def backward(l, grad, known=None):
+        relay("r", l)
+        second_grad = normalize_back_here(grad, "2", l, 1, known)
         b.sgb[l] = second_grad.astype(BF16)
         if l + 1 < LAYERS:
             to_owners("q", l + 1)
@@ -786,25 +913,33 @@
         piece = b.bg_all.at[l, pl.ds(g_rows, PART), :]
         for d in range(3):
             send(piece, piece, square[d], bg_sem[l] + d)
+        if known is not None:
+            norm_grads(grad, b.xh2[l], l, 1)
+        if l == 0:
+            send_norm_grads()
         grads = mm_nt(b.act[l], b.sgb[l])
-        b.gb_d[l] = grads.astype(BF16).reshape(8, PART_FF // 8, PART)
+        b.left[...] = grads[:, :128]
+        b.right[:, 0:64] = grads[:, 128:]
+        for i, part in enumerate(triples_from_rows(PART_FF // 2, b.left, b.right)):
+            b.raw[every(i, PART_FF // 2, 3), :] = part
+        b.gb_d[l] = b.raw[...].astype(BF16).reshape(8, FLAT, 128)
         to_sibling("d", l)
-        b.gb_u[l] = units_of(mm_nt(b.mid[l], b.eg[l]))
+        b.gb_u[l] = flat_units(mm_nt(b.mid[l], b.eg[l]))
         to_sibling("u", l)
         relayed("r", l)
-        for cg in range(4):
-            b.wn_r[l, cg] = rows_of(b.wr_in[l, :, cg])
+        wide_rows(b.wr_in[l], b.wn_r.at[l])
         for d, (fx, fy) in enumerate(((0, 1), (1, 0), (1, 1))):
             px = 1 - x if fx else x
             py = 1 - y if fy else y
             start = pl.multiple_of(PART * (2 * px + py), PART)
             arrived(b.bg_all.at[l, pl.ds(start, PART), :], bg_sem[l] + d)
-        attended_grad = sum(mm(b.wn_r[l, r], b.bg_all[l, PART * r : PART * (r + 1), :]) for r in range(4))
-        b.do_t[...] = attended_grad.astype(BF16)
         att = b.att_all[l, pl.ds(g_rows, PART), :]
-        for cg in range(4):
-            b.gb_o[l, :, cg] = units_of(mm_nt(att, b.bg_all[l, PART * cg : PART * (cg + 1), :]))
+        b.gb_o[l] = flat_units(mm_nt(att, b.bg_all[l]))
         to_sibling("o", l)
+        b.do_t[...] = mm(b.wn_r[l], b.bg_all[l]).astype(BF16)
+        to_owners("d", l)
+        to_owners("u", l)
+        to_owners("o", l)
 
         def one_head(h, carry):
             head = pl.multiple_of(HEAD * h, HEAD)
@@ -831,35 +966,29 @@
         b.gb_q[l, :, 1] = units_of(mm_nt(b.x_all[l], b.dk_t[...]))
         b.gb_q[l, :, 2] = units_of(mm_nt(b.x_all[l], b.dv_t[...]))
         to_sibling("q", l)
-        for name in "duo":
-            to_owners(name, l)
         here = mm(w_q, b.dq_t[...])
         here += mm(w_k, b.dk_t[:, pl.ds(own, HALF)]) + mm(w_v, b.dv_t[:, pl.ds(own, HALF)])
         arrived(b.dx_in.at[l], dx_sem[l])
         return b.fg[...] + here + b.dx_in[l]
 
-    arrived(b.cot_t, cot_sem)
-    position = lax.broadcasted_iota(jnp.int32, (PART, HALF), 1) + HALF * c
-    grad = jnp.where(position.astype(F32) < valid, b.cot_t[...].astype(F32), 0.0)
-    grad = backward(1, grad)
+    grad = backward(1, grad, (one, two))
     grad = backward(0, grad)
     send_back(grad, b.tg_out, b.tg_in, tg_sem)
     to_owners("q", 0)
 
-    gs_sem = new_sems()
-    for k in range(2):
-        for q in range(4):
-            send(
-                b.gs_acc.at[k, 48 * q : 48 * (q + 1), :], b.gs_in.at[2 * z + c],
-                (2 * k + g // 2, 4 * (g % 2) + q), gs_sem, True,
-            )
-
     arrived(b.mix_in, mix_sem)
     mixed[...] = b.mix_in[...].T
     for l in reversed(range(LAYERS)):
-        for name, out in (("d", g_down), ("u", g_up), ("o", g_out), ("q", g_qkv)):
-            arrived(getattr(b, "rg_" + name).at[l], owner_sem[name, l])
-            out[l] = sum(getattr(b, "rg_" + name)[l, i].astype(F32) for i in range(4))
+        for name, out in (("d", g_down), ("u", g_up), ("o", g_out)):
+            rg = getattr(b, "rg_" + name)
+            arrived(rg.at[l], owner_sem[name, l])
+            out[every(l, FLAT, 2), :] = sum(rg[l, i].astype(F32) for i in range(4))
+        arrived(b.rg_q.at[l], owner_sem["q", l])
+        total = sum(b.rg_q[l, i].astype(F32) for i in range(4))
+        b.left[0:72] = total[:, :UNIT].reshape(72, 128)
+        b.right[0:72] = total[:, UNIT:].reshape(72, 128)
+        for i, part in enumerate(triples_from_rows(36, b.left, b.right)):
+            g_qkv[every(l + 2 * i, 36, 6), :] = part
     arrived(b.tg_in, tg_sem)
     tokens_grad[...] = b.tg_in[...].T
     arrived(b.gs_in, gs_sem)
@@ -883,33 +1012,37 @@
 def fast_device(
     tokens, lengths, qkv_weight, out_weight, up_weight, down_weight, norm_gain, norm_shift, cotangent
 ):
-    length = jnp.full((8, 128), lengths[0], F32)
-    misc = jnp.stack([norm_gain[0], norm_shift[0], norm_gain[1], norm_shift[1]], axis=1)
-    misc = jnp.pad(misc, ((0, 0), (0, 124)))
+    def raw(array):
+        return array.reshape(LAYERS, -1, 128).transpose(1, 0, 2).reshape(-1, 128)
+
+    def unraw(array):
+        return array.reshape(-1, LAYERS, 128).transpose(1, 0, 2).reshape(LAYERS, -1)
+
     operands = (
         tokens[0],
         cotangent[0],
-        length,
-        misc,
-        qkv_weight.reshape(LAYERS, 3, UNIT, PART),
-        out_weight.reshape(LAYERS, UNIT, GROUPS, PART).transpose(0, 2, 1, 3),
-        up_weight.reshape(LAYERS, UNIT, PART_FF),
-        down_weight.reshape(LAYERS, PART_FF // 8, PART),
+        lengths,
+        norm_gain,
+        norm_shift,
+        raw(qkv_weight),
+        raw(out_weight),
+        raw(up_weight),
+        raw(down_weight),
     )
     vmem = pl.BlockSpec(memory_space=pltpu.VMEM)
     shapes = (
         ((ROWS, D), BF16),
         ((ROWS, D), BF16),
-        ((LAYERS, 3, UNIT, PART), F32),
-        ((LAYERS, GROUPS, UNIT, PART), F32),
-        ((LAYERS, UNIT, PART_FF), F32),
-        ((LAYERS, PART_FF // 8, PART), F32),
-        ((PART // 4, 128), F32),
+        ((3 * LAYERS * 36, 128), F32),
+        ((LAYERS * FLAT, 128), F32),
+        ((LAYERS * FLAT, 128), F32),
+        ((LAYERS * FLAT, 128), F32),
+        ((8, 128), F32),
     )
     mixed, tokens_grad, g_qkv, g_out, g_up, g_down, g_norm = pl.pallas_call(
         fast_kernel,
         out_shape=tuple(jax.ShapeDtypeStruct(*shape) for shape in shapes),
-        in_specs=[vmem] * len(operands),
+        in_specs=[vmem] * 2 + [pl.BlockSpec(memory_space=pltpu.SMEM)] + [vmem] * 6,
         out_specs=tuple([vmem] * len(shapes)),
         scratch_shapes=[pltpu.SemaphoreType.DMA((SEMS,))] + [pltpu.VMEM(*entry) for entry in SCRATCH.values()],
         compiler_params=pltpu.CompilerParams(
@@ -917,14 +1050,14 @@
         ),
         name="encoder",
     )(*operands)
-    g_norm = g_norm[:, :4].T
+    g_norm = g_norm[:4, :48]
     return (
         mixed[None],
         tokens_grad[None],
-        g_qkv.reshape(LAYERS, -1),
-        g_out.transpose(0, 2, 1, 3).reshape(LAYERS, -1),
-        g_up.reshape(LAYERS, -1),
-        g_down.reshape(LAYERS, -1),
+        unraw(g_qkv),
+        unraw(g_out),
+        unraw(g_up),
+        unraw(g_down),
         g_norm[0::2],
         g_norm[1::2],
     )

time: 182 us -> 155 us (0.85)
  Pallas kernels: 168 us -> 144 us
  local copies, waits for them, and re-layouts: 12.9 us -> 9.57 us
    pallas_call x1, Pallas kernels: 168 us -> 144 us  [fast_device(): pl.pallas_call(fast_kernel, out_shape=tuple((jax.ShapeDtypeStruct(*shape)...]
    reshape x7 -> x2, local copies, waits for them, and re-layouts: 4.79 us -> 1.8 us  [the longest x1 0.94 us: unraw(): return array.reshape(-1, LAYERS, 128).transpose(1, 0, 2).reshape(LAYERS, -1)]
    unnamed x26 -> x16, local copies, waits for them, and re-layouts: 5.05 us -> 5.27 us
where the time goes in v2:
time: 155 us
  Pallas kernels  144 us (93%)
  local copies, waits for them, and re-layouts  9.57 us (6%)
    pallas_call x1, Pallas kernels, fast_device(): pl.pallas_call(fast_kernel, out_shape=tuple((jax.ShapeDtypeStruct(*shape)...  144 us
    unnamed x16, local copies, waits for them, and re-layouts  5.27 us

profile of v2, /device:TPU:0, one launch (start us, length us, event | category | flops | bytes accessed | tf_op | source)
XLA Modules:
  0.0 154.5 jit_solution(7446290768926951905)
XLA Ops:
  0.6 0.9 reshape.64
  1.5 0.7 copy.25
  2.8 143.7 %encoder.1 = (bf16[128,768]{1,0:T(8,128)(2,1)}, bf16[128,768]{1,0:T(8,128)(2,1)}, f32[216,128]{1,0:T(8,128)}, f32[288,128]{1,0:T(8,128)}, f32[288,128]{1,0:T(8,1...) custom-call(bf16[128,768]{1,0:T(8,128)(2,1)} %bitcast.49, bf16[128,768]{1,0:T(8,128)(2,1)} %bitcast.50, s32[1]{0:T(128)S(6)} %copy.43.length, ...), custom_call_target="tpu_custom_call" | custom-call | tf_op jit(solution)/shard_map/encoder/pallas_call | solution.py:1042
  146.5 0.7 slice.9
  147.1 0.6 slice.10
  147.7 0.6 slice.11
  148.3 0.0 copy-start.1
  148.3 0.9 copy.36
  149.3 0.7 copy.37
  150.0 0.0 copy-done.1
  150.0 0.0 copy-start
  150.0 0.7 copy.44
  150.6 0.3 copy-done
  151.0 0.0 copy-start.4
  151.0 0.7 copy.45
  151.6 0.3 copy-done.4
  151.9 0.0 copy-start.3
  151.9 0.7 copy.46
  152.6 0.3 copy-done.3
  152.9 0.0 copy-start.2
  152.9 0.7 copy.47
  153.6 0.3 copy-done.2
  153.9 0.7 copy.48
Async XLA Ops:
  148.3 1.7 %copy-start.1 = (bf16[128,768]{1,0:T(8,128)(2,1)S(1)}, bf16[128,768]{1,0:T(8,128)(2,1)}, u32[]{:S(2)}) copy-start(bf16[128,768]{1,0:T(8,128)(2,1)} %get-tuple-element.15) | copy-start | bytes 589828
  150.0 1.0 copy-start
  151.0 1.0 copy-start.4
  151.9 1.0 copy-start.3
  152.9 1.0 copy-start.2

commit v3 on v2

--- a/solution.py
+++ b/solution.py
@@ -311,6 +311,9 @@
 NDEV = 32
 UNIT = PART // 8
 FLAT = UNIT * PART_FF // 128
+COLS_AT = 2 * FLAT
+ROWS_AT = COLS_AT + GROUPS * 2 * UNIT
+SHARD = ROWS_AT + FLAT
 HEADS_HERE = HEADS // GROUPS
 KEY_BLOCK = 256
 FF_BLOCK = 128
@@ -329,11 +332,9 @@
     wq_out=((LAYERS, 3, 2 * UNIT, 128), BF16),
     wc_out=((LAYERS, GROUPS, 2 * UNIT, 128), BF16),
     wr_out=((LAYERS, FLAT, 128), BF16),
-    wm_out=((LAYERS, 2, FLAT, 128), BF16),
+    wm_out=((LAYERS, 2 * FLAT, 128), BF16),
     wq_in=((LAYERS, 3, 8, 2 * UNIT, 128), BF16),
-    wc_in=((LAYERS, GROUPS, 8, 2 * UNIT, 128), BF16),
-    wr_in=((LAYERS, 8, FLAT, 128), BF16),
-    wm_in=((LAYERS, 8, 2, FLAT, 128), BF16),
+    w_in=((LAYERS, 2, 4, SHARD, 128), BF16),
     raw=((8 * FLAT, 128), F32),
     left=((PART_FF, 128), F32),
     right=((PART_FF, 128), F32),
@@ -371,7 +372,7 @@
     dv_t=((PART, FULL), BF16),
     dx_out=((LAYERS, PART, HALF), F32),
     dx_in=((LAYERS, PART, HALF), F32),
-    stats=((4 * LAYERS, 4, 8, HALF), F32),
+    stats=((4 * LAYERS, 4, 16, 128), F32),
     mix_out=((PART, HALF), BF16),
     mix_in=((D, ROWS), BF16),
     tg_out=((PART, HALF), BF16),
@@ -379,21 +380,21 @@
     gs_acc=((2, PART, 128), F32),
     gs_out=((2, 4, 8, 128), F32),
     gs_in=((8, 8, 128), F32),
-    gb_d=((LAYERS, 8, FLAT, 128), BF16),
-    gb_u=((LAYERS, 8, FLAT, 128), BF16),
-    gb_o=((LAYERS, 8, FLAT, 128), BF16),
+    gb_m=((LAYERS, 2, 4, 2 * FLAT, 128), BF16),
+    gb_o=((LAYERS, 2, 4, FLAT, 128), BF16),
     gb_q=((LAYERS, 8, 3, 2 * UNIT, 128), BF16),
-    sb_d=((LAYERS, 4, FLAT, 128), BF16),
-    sb_u=((LAYERS, 4, FLAT, 128), BF16),
+    sb_m=((LAYERS, 4, 2 * FLAT, 128), BF16),
     sb_o=((LAYERS, 4, FLAT, 128), BF16),
     sb_q=((LAYERS, 4, 3, 2 * UNIT, 128), BF16),
-    gm_d=((LAYERS, 4, FLAT, 128), BF16),
-    gm_u=((LAYERS, 4, FLAT, 128), BF16),
+    gm_m=((LAYERS, 4, 2 * FLAT, 128), BF16),
     gm_o=((LAYERS, 4, FLAT, 128), BF16),
     gm_q=((LAYERS, 4, 3, 2 * UNIT, 128), BF16),
-    rg_d=((LAYERS, 4, FLAT, 128), BF16),
-    rg_u=((LAYERS, 4, FLAT, 128), BF16),
-    rg_o=((LAYERS, 4, FLAT, 128), BF16),
+    rz_m=((LAYERS, 4, 2 * FLAT, 128), BF16),
+    rz_o=((LAYERS, 4, FLAT, 128), BF16),
+    gf_m=((LAYERS, 2 * FLAT, 128), BF16),
+    gf_o=((LAYERS, FLAT, 128), BF16),
+    rg_m=((LAYERS, 2 * FLAT, 128), BF16),
+    rg_o=((LAYERS, FLAT, 128), BF16),
     rg_q=((LAYERS, 4, 3, 2 * UNIT, 128), BF16),
 )
 
@@ -526,7 +527,8 @@
     norm_rows = jnp.concatenate([norm_rows, jnp.zeros((8, 80), F32)], axis=1)
     norm_rows = jnp.concatenate([norm_rows, jnp.zeros((120, 128), F32)], axis=0)
     b.misc[...] = norm_rows.T.astype(BF16)
-    b.raw[0:216] = w_qkv[...].astype(F32)
+    for k in range(108):
+        b.raw[2 * k : 2 * k + 2] = w_qkv[:, 128 * k : 128 * (k + 1)].astype(F32)
     for l in range(LAYERS):
         rows_from_triples(*(b.raw[every(l + 2 * i, 36, 6), :] for i in range(3)), b.left, b.right)
         for k in range(3):
@@ -563,9 +565,12 @@
 
         pending.append((copy, jnp.logical_and(first_chunk, away)))
 
-    weights_in = dict(q=b.wq_in, r=b.wr_in, c=b.wc_in, m=b.wm_in)
-    arrive_w = {(name, l): new_sems() for l in range(LAYERS) for name in "qrcm"}
-    relay_w = {(name, l): new_sems() for l in range(LAYERS) for name in "qrcm"}
+    arrive_q = [new_sems() for _ in range(LAYERS)]
+    relay_q = [new_sems() for _ in range(LAYERS)]
+    level_w = [new_sems() for _ in range(LAYERS)]
+    PARTS = dict(c=(COLS_AT, ROWS_AT - COLS_AT), m=(0, COLS_AT), r=(ROWS_AT, FLAT))
+    along_w = {(name, l): new_sems(3) for l in range(LAYERS) for name in PARTS}
+    relay_w = {(name, l): new_sems() for l in range(LAYERS) for name in PARTS}
 
     def send_qkv(l):
         for k in range(3):
@@ -574,37 +579,42 @@
             for zz in range(4):
                 send(
                     b.wq_out.at[l, k], b.wq_in.at[l, cc, t],
-                    dev(gg // 2, t // 4, zz, gg % 2), arrive_w["q", l], True,
+                    dev(gg // 2, t // 4, zz, gg % 2), arrive_q[l], True,
                 )
 
-    def send_columns(l):
+    def relay_qkv(l):
+        mine = b.wq_in.at[l, :, pl.ds(4 * c, 4)]
+        arrived(mine, arrive_q[l])
+        send(mine, mine, sibling, relay_q[l])
+
+    def send_level(l):
+        to = dev(p // 2, y, z, p % 2)
+        into = b.w_in.at[l, y, z]
+        send(b.wm_out.at[l], into.at[0:COLS_AT], to, level_w[l], True)
         for cg in range(4):
-            for zz in range(4):
-                send(
-                    b.wc_out.at[l, cg], b.wc_in.at[l, p, s],
-                    dev(cg // 2, s // 4, zz, cg % 2), arrive_w["c", l], True,
-                )
-
-    def send_rows(l):
-        for zz in range(4):
-            send(b.wr_out.at[l], b.wr_in.at[l, s], dev(p // 2, s // 4, zz, p % 2), arrive_w["r", l], True)
-
-    def send_updown(l):
-        for zz in range(4):
-            send(b.wm_out.at[l], b.wm_in.at[l, s], dev(p // 2, s // 4, zz, p % 2), arrive_w["m", l], True)
-
-    def half(name, l, which):
-        ref = weights_in[name]
-        units = pl.ds(4 * which, 4)
-        return ref.at[l, :, units] if name in "qc" else ref.at[l, units]
+            row = pl.multiple_of(COLS_AT + 2 * UNIT * p, 16)
+            send(b.wc_out.at[l, cg], into.at[pl.ds(row, 2 * UNIT)], dev(cg // 2, y, z, cg % 2), level_w[l], True)
+        send(b.wr_out.at[l], into.at[ROWS_AT:SHARD], to, level_w[l], True)
+
+    def level_here(l):
+        arrived(b.w_in.at[l, c, z], level_w[l])
+
+    def send_along(name, l):
+        start, count = PARTS[name]
+        piece = b.w_in.at[l, c, z, start : start + count]
+        for i in range(3):
+            send(piece, piece, dev(x, c, (z + i + 1) % 4, y), along_w[name, l] + i)
 
     def relay(name, l):
-        mine = half(name, l, c)
-        arrived(mine, arrive_w[name, l])
+        start, count = PARTS[name]
+        for i in range(3):
+            arrived(b.w_in.at[l, c, (z + 3 - i) % 4, start : start + count], along_w[name, l] + i)
+        mine = b.w_in.at[l, c, :, start : start + count]
         send(mine, mine, sibling, relay_w[name, l])
 
     def relayed(name, l):
-        arrived(half(name, l, 1 - c), relay_w[name, l])
+        start, count = PARTS[name]
+        arrived(b.w_in.at[l, 1 - c, :, start : start + count], relay_w[name, l])
 
     send_qkv(0)
     for zz in range(4):
@@ -631,15 +641,18 @@
     for i, ref in enumerate((w_up, w_down)):
         b.raw[0:288] = ref[...].astype(F32)
         for l in range(LAYERS):
-            b.wm_out[l, i] = b.raw[every(l, FLAT, 2), :].astype(BF16)
-
+            b.wm_out[l, FLAT * i : FLAT * (i + 1)] = b.raw[every(l, FLAT, 2), :].astype(BF16)
+
+    send_level(0)
+    send_level(1)
+    level_here(0)
     x_sem = [new_sems() for _ in range(LAYERS)]
     x_half = b.x_all.at[0, :, pl.ds(own, HALF)]
     arrived(x_half, tok_sem)
     send(x_half, x_half, sibling, x_sem[0])
-    relay("q", 0)
-    send_columns(0)
-    send_updown(0)
+    send_along("c", 0)
+    send_along("m", 0)
+    relay_qkv(0)
     arrived(b.ln_in, len_sem)
     valid = b.ln_in[0:1, 0:1]
     key_at = lax.broadcasted_iota(jnp.int32, (FULL, 128), 0).astype(F32)
@@ -656,15 +669,25 @@
         i = stat_used[0]
         stat_used[0] += 1
         buffer = b.stats.at[i]
-        buffer[0] = jnp.concatenate([*rows, jnp.zeros((8 - len(rows), HALF), F32)], axis=0)
+        count = 4 * len(rows)
+        buffer[0, 0:count] = jnp.concatenate(
+            [row[:, ROWS * j : ROWS * (j + 1)] for row in rows for j in range(4)], axis=0
+        )
         base = new_sems(3)
         for d in range(3):
-            send(buffer.at[0], buffer.at[d + 1], square[d], base + d)
+            send(buffer.at[0, 0:count], buffer.at[d + 1, 0:count], square[d], base + d)
 
         def finish():
             for d in range(3):
-                arrived(buffer.at[d + 1], base + d)
-            return [[buffer[d, i : i + 1] for i in range(len(rows))] for d in range(4)]
+                arrived(buffer.at[d + 1, 0:count], base + d)
+            whole = [buffer[d, 0:count] for d in range(4)]
+            return [
+                [
+                    jnp.concatenate([four[4 * i + j : 4 * i + j + 1] for j in range(4)], axis=1)
+                    for i in range(len(rows))
+                ]
+                for four in whole
+            ]
 
         return finish
 
@@ -691,15 +714,23 @@
         two = sum(f[3] + (f[0] - mean) * f[2] for f in four) * factor * (1.0 / D)
         return result, one, two
 
-    def wide_rows(units, into):
-        b.raw[...] = units.astype(F32).reshape(8 * FLAT, 128)
+    def gather_raw(l, start):
+        for t in range(8):
+            b.raw[FLAT * t : FLAT * (t + 1)] = b.w_in[l, t % 2, t // 2, start : start + FLAT].astype(F32)
+
+    def wide_rows(l, start, into):
+        gather_raw(l, start)
         for i in range(6):
             into[:, 128 * i : 128 * (i + 1)] = b.raw[every(i, PART, 6), :].astype(BF16)
 
-    def flat_units(matrix):
+    def scatter_raw(ref, start):
+        for t in range(8):
+            ref[t % 2, t // 2, start : start + FLAT] = b.raw[FLAT * t : FLAT * (t + 1)].astype(BF16)
+
+    def flat_units(matrix, ref, start):
         for i in range(6):
             b.raw[every(i, PART, 6), :] = matrix[:, 128 * i : 128 * (i + 1)]
-        return b.raw[...].astype(BF16).reshape(8, FLAT, 128)
+        scatter_raw(ref, start)
 
     att_sem = [[new_sems(3) for _ in range(3)] for _ in range(LAYERS)]
     att_send = [[new_sems(3) for _ in range(3)] for _ in range(LAYERS)]
@@ -714,7 +745,7 @@
 
     def forward(l):
         x_own = b.x_all[l, :, pl.ds(own, HALF)]
-        relayed("q", l)
+        arrived(b.wq_in.at[l, :, pl.ds(4 * (1 - c), 4)], relay_q[l])
         turned = []
         for cc in range(3):
             nat = matrix_of(b.wq_in[l, cc])
@@ -763,7 +794,14 @@
         lax.fori_loop(0, HEADS_HERE, one_head, 0)
         relay("c", l)
         relayed("c", l)
-        columns_t = matrix_of(b.wc_in[l].reshape(32, 2 * UNIT, 128)).T
+        for r in range(4):
+            for t in range(8):
+                rows = slice(UNIT * (8 * r + t), UNIT * (8 * r + t + 1))
+                start = COLS_AT + 2 * UNIT * r
+                unit = b.w_in[l, t % 2, t // 2, start : start + 2 * UNIT].astype(F32)
+                b.left[rows] = unit[:UNIT]
+                b.right[rows] = unit[UNIT:]
+        columns_t = jnp.concatenate([b.left[...], b.right[:, 0:64]], axis=1).astype(BF16).T
         flips = ((0, 1), (1, 0), (1, 1))
         for h in range(HEADS_HERE):
             for d, (fx, fy) in enumerate(flips):
@@ -776,9 +814,9 @@
         gain, shift = gain_shift(l, 0)
         finish = normalize_here(x_own.astype(F32) + branch, "1", l, gain, shift)
         relayed("m", l)
-        wide_rows(b.wm_in[l, :, 0], b.wn_u.at[l])
+        wide_rows(l, 0, b.wn_u.at[l])
         b.wt_u[...] = b.wn_u[l].T
-        b.raw[...] = b.wm_in[l, :, 1].astype(F32).reshape(8 * FLAT, 128)
+        gather_raw(l, FLAT)
         rows_from_triples(*(b.raw[every(i, PART_FF // 2, 3), :] for i in range(3)), b.left, b.right)
         nat = jnp.concatenate([b.left[...], b.right[:, 0:64]], axis=1).astype(BF16)
         b.wn_d[l] = nat
@@ -786,6 +824,9 @@
         middle = finish().astype(BF16)
         if l == 0:
             send_qkv(1)
+            level_here(1)
+            send_along("c", 1)
+            send_along("m", 1)
             send_cotangent()
         b.mid[l] = middle
 
@@ -811,11 +852,9 @@
     b.x_all[1, :, pl.ds(own, HALF)] = hidden.astype(BF16)
     x_half = b.x_all.at[1, :, pl.ds(own, HALF)]
     send(x_half, x_half, sibling, x_sem[1])
-    relay("q", 1)
-    send_columns(1)
-    send_updown(1)
-    send_rows(1)
-    send_rows(0)
+    relay_qkv(1)
+    send_along("r", 1)
+    send_along("r", 0)
     (hidden, one, two), grad = forward(1)
 
     mix_sem, tg_sem = new_sems(), new_sems()
@@ -830,25 +869,39 @@
 
     send_back(hidden, b.mix_out, b.mix_in, mix_sem)
 
-    half_sem = {(name, l): new_sems() for l in range(LAYERS) for name in "duoq"}
-    owner_sem = {(name, l): new_sems() for l in range(LAYERS) for name in "duoq"}
+    half_sem = {(name, l): new_sems() for l in range(LAYERS) for name in "moq"}
+    level_sem = {(name, l): new_sems(3) for l in range(LAYERS) for name in "mo"}
+    owner_sem = {(name, l): new_sems() for l in range(LAYERS) for name in "moq"}
 
     def to_sibling(name, l):
-        send(
-            getattr(b, "gb_" + name).at[l, pl.ds(4 * (1 - c), 4)], getattr(b, "sb_" + name).at[l], sibling, half_sem[name, l]
-        )
-
-    def to_owners(name, l):
-        arrived(getattr(b, "sb_" + name).at[l], half_sem[name, l])
-        mine = getattr(b, "gb_" + name)[l, pl.ds(4 * c, 4)].astype(F32) + getattr(b, "sb_" + name)[l].astype(F32)
-        getattr(b, "gm_" + name)[l] = mine.astype(BF16)
+        there = pl.ds(4 * (1 - c), 4) if name == "q" else 1 - c
+        send(getattr(b, "gb_" + name).at[l, there], getattr(b, "sb_" + name).at[l], sibling, half_sem[name, l])
+
+    def to_level(name, l):
+        here, mine = getattr(b, "sb_" + name), getattr(b, "gm_" + name)
+        arrived(here.at[l], half_sem[name, l])
+        mine[l] = (getattr(b, "gb_" + name)[l, c].astype(F32) + here[l].astype(F32)).astype(BF16)
+        for i in range(3):
+            there = (z + i + 1) % 4
+            send(
+                mine.at[l, there], getattr(b, "rz_" + name).at[l, i], dev(x, c, there, y), level_sem[name, l] + i
+            )
+
+    def to_owner(name, l):
+        four = getattr(b, "rz_" + name)
+        for i in range(3):
+            arrived(four.at[l, i], level_sem[name, l] + i)
+        total = getattr(b, "gm_" + name)[l, z].astype(F32) + sum(four[l, i].astype(F32) for i in range(3))
+        final = getattr(b, "gf_" + name)
+        final[l] = total.astype(BF16)
+        send(final.at[l], getattr(b, "rg_" + name).at[l], dev(g // 2, g % 2, z, c), owner_sem[name, l], True)
+
+    def qkv_to_owners(l):
+        arrived(b.sb_q.at[l], half_sem["q", l])
+        b.gm_q[l] = (b.gb_q[l, pl.ds(4 * c, 4)].astype(F32) + b.sb_q[l].astype(F32)).astype(BF16)
         for k in range(4):
-            t = 4 * c + k
-            if name != "q":
-                send(getattr(b, "gm_" + name).at[l, k], getattr(b, "rg_" + name).at[l, z], (g, t), owner_sem[name, l], True)
-                continue
             for cc in range(3):
-                u = 32 * cc + 8 * g + t
+                u = 32 * cc + 8 * g + 4 * c + k
                 j = u // 3
                 send(
                     b.gm_q.at[l, k, cc], b.rg_q.at[l, z, u % 3], (j // 8, j % 8), owner_sem["q", l], True
@@ -897,7 +950,7 @@
         second_grad = normalize_back_here(grad, "2", l, 1, known)
         b.sgb[l] = second_grad.astype(BF16)
         if l + 1 < LAYERS:
-            to_owners("q", l + 1)
+            qkv_to_owners(l + 1)
 
         def one_block(i, carry):
             rows = pl.ds(pl.multiple_of(FF_BLOCK * i, FF_BLOCK), FF_BLOCK)
@@ -922,24 +975,25 @@
         b.right[:, 0:64] = grads[:, 128:]
         for i, part in enumerate(triples_from_rows(PART_FF // 2, b.left, b.right)):
             b.raw[every(i, PART_FF // 2, 3), :] = part
-        b.gb_d[l] = b.raw[...].astype(BF16).reshape(8, FLAT, 128)
-        to_sibling("d", l)
-        b.gb_u[l] = flat_units(mm_nt(b.mid[l], b.eg[l]))
-        to_sibling("u", l)
+        scatter_raw(b.gb_m.at[l], 0)
+        flat_units(mm_nt(b.mid[l], b.eg[l]), b.gb_m.at[l], FLAT)
+        to_sibling("m", l)
+        if l + 1 < LAYERS:
+            to_owner("m", l + 1)
+            to_owner("o", l + 1)
         relayed("r", l)
-        wide_rows(b.wr_in[l], b.wn_r.at[l])
+        wide_rows(l, ROWS_AT, b.wn_r.at[l])
         for d, (fx, fy) in enumerate(((0, 1), (1, 0), (1, 1))):
             px = 1 - x if fx else x
             py = 1 - y if fy else y
             start = pl.multiple_of(PART * (2 * px + py), PART)
             arrived(b.bg_all.at[l, pl.ds(start, PART), :], bg_sem[l] + d)
         att = b.att_all[l, pl.ds(g_rows, PART), :]
-        b.gb_o[l] = flat_units(mm_nt(att, b.bg_all[l]))
+        flat_units(mm_nt(att, b.bg_all[l]), b.gb_o.at[l], 0)
         to_sibling("o", l)
         b.do_t[...] = mm(b.wn_r[l], b.bg_all[l]).astype(BF16)
-        to_owners("d", l)
-        to_owners("u", l)
-        to_owners("o", l)
+        to_level("m", l)
+        to_level("o", l)
 
         def one_head(h, carry):
             head = pl.multiple_of(HEAD * h, HEAD)
@@ -974,25 +1028,31 @@
     grad = backward(1, grad, (one, two))
     grad = backward(0, grad)
     send_back(grad, b.tg_out, b.tg_in, tg_sem)
-    to_owners("q", 0)
+    qkv_to_owners(0)
+    to_owner("m", 0)
+    to_owner("o", 0)
 
     arrived(b.mix_in, mix_sem)
     mixed[...] = b.mix_in[...].T
     for l in reversed(range(LAYERS)):
-        for name, out in (("d", g_down), ("u", g_up), ("o", g_out)):
-            rg = getattr(b, "rg_" + name)
-            arrived(rg.at[l], owner_sem[name, l])
-            out[every(l, FLAT, 2), :] = sum(rg[l, i].astype(F32) for i in range(4))
+        arrived(b.rg_m.at[l], owner_sem["m", l])
+        g_down[every(l, FLAT, 2), :] = b.rg_m[l, 0:FLAT].astype(F32)
+        g_up[every(l, FLAT, 2), :] = b.rg_m[l, FLAT : 2 * FLAT].astype(F32)
+        arrived(b.rg_o.at[l], owner_sem["o", l])
+        g_out[every(l, FLAT, 2), :] = b.rg_o[l].astype(F32)
         arrived(b.rg_q.at[l], owner_sem["q", l])
         total = sum(b.rg_q[l, i].astype(F32) for i in range(4))
         b.left[0:72] = total[:, :UNIT].reshape(72, 128)
         b.right[0:72] = total[:, UNIT:].reshape(72, 128)
         for i, part in enumerate(triples_from_rows(36, b.left, b.right)):
-            g_qkv[every(l + 2 * i, 36, 6), :] = part
+            b.raw[every(l + 2 * i, 36, 6), :] = part
     arrived(b.tg_in, tg_sem)
     tokens_grad[...] = b.tg_in[...].T
     arrived(b.gs_in, gs_sem)
     g_norm[...] = sum(b.gs_in[i] for i in range(8))
+
+    for k in range(108):
+        g_qkv[:, 128 * k : 128 * (k + 1)] = b.raw[2 * k : 2 * k + 2]
 
     for copy, when in pending:
         if when is None:
@@ -1009,6 +1069,15 @@
                 ).wait_send()
 
 
+def hand_over(*refs):
+    plain, norms, outs = refs[:6], refs[6], refs[7:]
+    for ref, out in zip(plain, outs):
+        out[...] = ref[...]
+    for k in range(2):
+        for l in range(LAYERS):
+            outs[6 + k][l : l + 1, :] = norms[2 * l + k : 2 * l + k + 1, 0 : PART // 4]
+
+
 def fast_device(
     tokens, lengths, qkv_weight, out_weight, up_weight, down_weight, norm_gain, norm_shift, cotangent
 ):
@@ -1024,7 +1093,7 @@
         lengths,
         norm_gain,
         norm_shift,
-        raw(qkv_weight),
+        qkv_weight,
         raw(out_weight),
         raw(up_weight),
         raw(down_weight),
@@ -1033,7 +1102,7 @@
     shapes = (
         ((ROWS, D), BF16),
         ((ROWS, D), BF16),
-        ((3 * LAYERS * 36, 128), F32),
+        ((LAYERS, 3 * UNIT * PART), F32),
         ((LAYERS * FLAT, 128), F32),
         ((LAYERS * FLAT, 128), F32),
         ((LAYERS * FLAT, 128), F32),
@@ -1050,16 +1119,25 @@
         ),
         name="encoder",
     )(*operands)
-    g_norm = g_norm[:4, :48]
+    results = (mixed, tokens_grad, g_qkv, g_out, g_up, g_down)
+    shapes = [jax.ShapeDtypeStruct(array.shape, array.dtype) for array in results]
+    shapes += [jax.ShapeDtypeStruct((LAYERS, PART // 4), F32)] * 2
+    mixed, tokens_grad, g_qkv, g_out, g_up, g_down, g_gain, g_shift = pl.pallas_call(
+        hand_over,
+        out_shape=tuple(shapes),
+        in_specs=[vmem] * (len(results) + 1),
+        out_specs=tuple([vmem] * len(shapes)),
+        name="hand_over",
+    )(*results, g_norm)
     return (
         mixed[None],
         tokens_grad[None],
-        unraw(g_qkv),
+        g_qkv,
         unraw(g_out),
         unraw(g_up),
         unraw(g_down),
-        g_norm[0::2],
-        g_norm[1::2],
+        g_gain,
+        g_shift,
     )
 
 

time: 155 us -> 141 us (0.910)
  local copies, waits for them, and re-layouts: 9.57 us -> 0 us
  Pallas kernels: 144 us -> 139 us
    pallas_call x1, Pallas kernels: 144 us -> 137 us  [fast_device(): pl.pallas_call(fast_kernel, out_shape=tuple((jax.ShapeDtypeStruct(*shape)...]
    unnamed x16 -> x0, local copies, waits for them, and re-layouts: 5.27 us -> none
    pallas_call x0 -> x1, Pallas kernels: none -> 2.23 us  [fast_device(): pl.pallas_call(hand_over, out_shape=tuple(shapes), in_specs=[vmem] * (len...]
    slice x3 -> x0, local copies, waits for them, and re-layouts: 1.84 us -> none  [the longest x1 0.68 us: fast_device(): g_norm = g_norm[:4, :48]]
    reshape x2 -> x0, local copies, waits for them, and re-layouts: 1.8 us -> none  [the longest x1 0.94 us: unraw(): return array.reshape(-1, LAYERS, 128).transpose(1, 0, 2).reshape(LAYERS, -1)]
where the time goes in v3:
time: 141 us; the launch traced here: 140 us
  Pallas kernels  139 us (99%)
    pallas_call x1, Pallas kernels, fast_device(): pl.pallas_call(fast_kernel, out_shape=tuple((jax.ShapeDtypeStruct(*shape)...  137 us

profile of v3, /device:TPU:0, one launch (start us, length us, event | category | flops | bytes accessed | tf_op | source)
XLA Modules:
  0.0 140.3 jit_solution(4350906605274984618)
XLA Ops:
  1.3 136.7 %encoder.1 = (bf16[128,768]{1,0:T(8,128)(2,1)}, bf16[128,768]{1,0:T(8,128)(2,1)}, f32[2,13824]{1,0:T(2,128)}, f32[288,128]{1,0:T(8,128)}, f32[288,128]{1,0:T(8,1...) custom-call(bf16[128,768]{1,0:T(8,128)(2,1)} %bitcast.34, bf16[128,768]{1,0:T(8,128)(2,1)} %bitcast.35, s32[1]{0:T(128)S(6)} %copy.23.length, ...), custom_call_target="tpu_custom_call" | custom-call | tf_op jit(solution)/shard_map/encoder/pallas_call | solution.py:1111
  138.0 2.2 %hand_over.1 = (bf16[128,768]{1,0:T(8,128)(2,1)}, bf16[128,768]{1,0:T(8,128)(2,1)}, f32[2,13824]{1,0:T(2,128)}, f32[288,128]{1,0:T(8,128)}, f32[288,128]{1,0:T(8...) custom-call(bf16[128,768]{1,0:T(8,128)(2,1)} %get-tuple-element.23.refs_0_, ...), custom_call_target="tpu_custom_call" | custom-call | tf_op jit(solution)/shard_map/hand_over/pallas_call | solution.py:1125

commit v4 on v3

--- a/solution.py
+++ b/solution.py
@@ -313,7 +313,8 @@
 FLAT = UNIT * PART_FF // 128
 COLS_AT = 2 * FLAT
 ROWS_AT = COLS_AT + GROUPS * 2 * UNIT
-SHARD = ROWS_AT + FLAT
+QKV_AT = ROWS_AT + FLAT
+SHARD = QKV_AT + 3 * 2 * UNIT
 HEADS_HERE = HEADS // GROUPS
 KEY_BLOCK = 256
 FF_BLOCK = 128
@@ -321,6 +322,14 @@
 MESH = pl.DeviceIdType.MESH
 
 SCRATCH = dict(
+    tokens=((ROWS, D), BF16),
+    w_qkv=((LAYERS, 3 * UNIT * PART), BF16),
+    gains=((LAYERS, PART // 4), BF16),
+    shifts=((LAYERS, PART // 4), BF16),
+    w_out=((LAYERS * FLAT, 128), BF16),
+    w_up=((LAYERS * FLAT, 128), BF16),
+    w_down=((LAYERS * FLAT, 128), BF16),
+    cotangent=((ROWS, D), BF16),
     x_all=((LAYERS, PART, FULL), BF16),
     cot_t=((PART, HALF), BF16),
     tok_t=((D, ROWS), BF16),
@@ -333,7 +342,6 @@
     wc_out=((LAYERS, GROUPS, 2 * UNIT, 128), BF16),
     wr_out=((LAYERS, FLAT, 128), BF16),
     wm_out=((LAYERS, 2 * FLAT, 128), BF16),
-    wq_in=((LAYERS, 3, 8, 2 * UNIT, 128), BF16),
     w_in=((LAYERS, 2, 4, SHARD, 128), BF16),
     raw=((8 * FLAT, 128), F32),
     left=((PART_FF, 128), F32),
@@ -458,7 +466,7 @@
 
 
 def fast_kernel(
-    tokens, cotangent, length, gains, shifts, w_qkv, w_out, w_up, w_down,
+    tokens_at, cotangent_at, length, gains_at, shifts_at, w_qkv_at, w_out_at, w_up_at, w_down_at,
     mixed, tokens_grad, g_qkv, g_out, g_up, g_down, g_norm,
     sems, *scratch,
 ):
@@ -509,6 +517,18 @@
     def arrived(ref, arrive):
         pltpu.make_async_copy(ref, ref, sems.at[arrive]).wait()
 
+    reads = {}
+    for ref, into in (
+        (tokens_at, b.tokens), (w_qkv_at, b.w_qkv), (gains_at, b.gains), (shifts_at, b.shifts), (w_out_at, b.w_out),
+        (w_up_at, b.w_up), (w_down_at, b.w_down), (cotangent_at, b.cotangent),
+    ):
+        reads[id(into)] = pltpu.make_async_copy(ref, into, sems.at[new_sems()])
+        reads[id(into)].start()
+
+    def read(ref):
+        reads[id(ref)].wait()
+        return ref
+
     me = 8 * p + s
     barrier = pltpu.get_barrier_semaphore()
 
@@ -518,15 +538,9 @@
         return carry
 
     lax.fori_loop(1, NDEV, greet, 0)
-    b.tok_t[...] = tokens[...].T
-    b.cotown_t[...] = cotangent[...].T
-    b.gs_acc[...] = jnp.zeros((2, PART, 128), F32)
     b.ln_out[...] = jnp.full((8, 128), length[0].astype(F32), F32)
-    norm_rows = [ref[...].astype(F32)[l : l + 1] for l in range(LAYERS) for ref in (gains, shifts)]
-    norm_rows = jnp.concatenate(norm_rows + [jnp.zeros((4, 48), F32)], axis=0)
-    norm_rows = jnp.concatenate([norm_rows, jnp.zeros((8, 80), F32)], axis=1)
-    norm_rows = jnp.concatenate([norm_rows, jnp.zeros((120, 128), F32)], axis=0)
-    b.misc[...] = norm_rows.T.astype(BF16)
+    b.tok_t[...] = read(b.tokens)[...].T
+    w_qkv = read(b.w_qkv)
     for k in range(108):
         b.raw[2 * k : 2 * k + 2] = w_qkv[:, 128 * k : 128 * (k + 1)].astype(F32)
     for l in range(LAYERS):
@@ -536,8 +550,57 @@
             b.wq_out[l, k] = jnp.concatenate([b.left[rows], b.right[rows]], axis=0).astype(BF16)
     pl.semaphore_wait(barrier, NDEV - 1)
 
+    level_w = [new_sems() for _ in range(LAYERS)]
+    level_q = [new_sems() for _ in range(LAYERS)]
+    PARTS = dict(c=(COLS_AT, ROWS_AT - COLS_AT), m=(0, COLS_AT), r=(ROWS_AT, FLAT), q=(QKV_AT, SHARD - QKV_AT))
+    along_w = {(name, l): new_sems(3) for l in range(LAYERS) for name in PARTS}
+    relay_w = {(name, l): new_sems() for l in range(LAYERS) for name in PARTS}
+
+    def send_level(l):
+        to = dev(p // 2, y, z, p % 2)
+        into = b.w_in.at[l, y, z]
+        send(b.wm_out.at[l], into.at[0:COLS_AT], to, level_w[l], True)
+        for cg in range(4):
+            row = pl.multiple_of(COLS_AT + 2 * UNIT * p, 16)
+            send(b.wc_out.at[l, cg], into.at[pl.ds(row, 2 * UNIT)], dev(cg // 2, y, z, cg % 2), level_w[l], True)
+        send(b.wr_out.at[l], into.at[ROWS_AT:QKV_AT], to, level_w[l], True)
+
+    def send_level_qkv(l):
+        into = b.w_in.at[l, y, z]
+        for k in range(3):
+            gg = (3 * me + k) % 32 // 8
+            start = QKV_AT + 2 * UNIT * k
+            send(b.wq_out.at[l, k], into.at[start : start + 2 * UNIT], dev(gg // 2, y, z, gg % 2), level_q[l], True)
+
+    def level_here(l):
+        arrived(b.w_in.at[l, c, z, 0:QKV_AT], level_w[l])
+
+    def level_qkv_here(l):
+        arrived(b.w_in.at[l, c, z, QKV_AT:SHARD], level_q[l])
+
+    def send_along(name, l):
+        start, count = PARTS[name]
+        piece = b.w_in.at[l, c, z, start : start + count]
+        for i in range(3):
+            send(piece, piece, dev(x, c, (z + i + 1) % 4, y), along_w[name, l] + i)
+
+    def relay(name, l):
+        start, count = PARTS[name]
+        for i in range(3):
+            arrived(b.w_in.at[l, c, (z + 3 - i) % 4, start : start + count], along_w[name, l] + i)
+        mine = b.w_in.at[l, c, :, start : start + count]
+        send(mine, mine, sibling, relay_w[name, l])
+
+    def relayed(name, l):
+        start, count = PARTS[name]
+        arrived(b.w_in.at[l, 1 - c, :, start : start + count], relay_w[name, l])
+
+    def send_first():
+        send_level_qkv(0)
+
     tok_sem, len_sem, cot_sem, gn_sem = (new_sems() for _ in range(4))
     half_of = s // 4
+    send_first()
     for gg in range(4):
         to = dev(gg // 2, half_of, z_mine, gg % 2)
         lane = pl.multiple_of(ROWS * s, ROWS)
@@ -565,67 +628,15 @@
 
         pending.append((copy, jnp.logical_and(first_chunk, away)))
 
-    arrive_q = [new_sems() for _ in range(LAYERS)]
-    relay_q = [new_sems() for _ in range(LAYERS)]
-    level_w = [new_sems() for _ in range(LAYERS)]
-    PARTS = dict(c=(COLS_AT, ROWS_AT - COLS_AT), m=(0, COLS_AT), r=(ROWS_AT, FLAT))
-    along_w = {(name, l): new_sems(3) for l in range(LAYERS) for name in PARTS}
-    relay_w = {(name, l): new_sems() for l in range(LAYERS) for name in PARTS}
-
-    def send_qkv(l):
-        for k in range(3):
-            u = 3 * me + k
-            cc, gg, t = u // 32, (u % 32) // 8, u % 8
-            for zz in range(4):
-                send(
-                    b.wq_out.at[l, k], b.wq_in.at[l, cc, t],
-                    dev(gg // 2, t // 4, zz, gg % 2), arrive_q[l], True,
-                )
-
-    def relay_qkv(l):
-        mine = b.wq_in.at[l, :, pl.ds(4 * c, 4)]
-        arrived(mine, arrive_q[l])
-        send(mine, mine, sibling, relay_q[l])
-
-    def send_level(l):
-        to = dev(p // 2, y, z, p % 2)
-        into = b.w_in.at[l, y, z]
-        send(b.wm_out.at[l], into.at[0:COLS_AT], to, level_w[l], True)
-        for cg in range(4):
-            row = pl.multiple_of(COLS_AT + 2 * UNIT * p, 16)
-            send(b.wc_out.at[l, cg], into.at[pl.ds(row, 2 * UNIT)], dev(cg // 2, y, z, cg % 2), level_w[l], True)
-        send(b.wr_out.at[l], into.at[ROWS_AT:SHARD], to, level_w[l], True)
-
-    def level_here(l):
-        arrived(b.w_in.at[l, c, z], level_w[l])
-
-    def send_along(name, l):
-        start, count = PARTS[name]
-        piece = b.w_in.at[l, c, z, start : start + count]
-        for i in range(3):
-            send(piece, piece, dev(x, c, (z + i + 1) % 4, y), along_w[name, l] + i)
-
-    def relay(name, l):
-        start, count = PARTS[name]
-        for i in range(3):
-            arrived(b.w_in.at[l, c, (z + 3 - i) % 4, start : start + count], along_w[name, l] + i)
-        mine = b.w_in.at[l, c, :, start : start + count]
-        send(mine, mine, sibling, relay_w[name, l])
-
-    def relayed(name, l):
-        start, count = PARTS[name]
-        arrived(b.w_in.at[l, 1 - c, :, start : start + count], relay_w[name, l])
-
-    send_qkv(0)
-    for zz in range(4):
-        for cc in range(2):
-            gg = 2 * (p % 2) + s // 4
-            row = pl.multiple_of(48 * (s % 4), 16)
-            send(
-                b.misc.at[0:48, :], b.gn_in.at[p // 2, pl.ds(row, 48), :],
-                dev(gg // 2, cc, zz, gg % 2), gn_sem, True,
-            )
-    b.raw[0:288] = w_out[...].astype(F32)
+    gains, shifts = read(b.gains), read(b.shifts)
+    b.gs_acc[...] = jnp.zeros((2, PART, 128), F32)
+    norm_rows = [ref[...].astype(F32)[l : l + 1] for l in range(LAYERS) for ref in (gains, shifts)]
+    norm_rows = jnp.concatenate(norm_rows + [jnp.zeros((4, 48), F32)], axis=0)
+    norm_rows = jnp.concatenate([norm_rows, jnp.zeros((8, 80), F32)], axis=1)
+    norm_rows = jnp.concatenate([norm_rows, jnp.zeros((120, 128), F32)], axis=0)
+    b.misc[...] = norm_rows.T.astype(BF16)
+
+    b.raw[0:288] = read(b.w_out)[...].astype(F32)
     for l in range(LAYERS):
         b.wr_out[l] = b.raw[every(l, FLAT, 2), :].astype(BF16)
         parts = [b.raw[every(2 * i + l, UNIT, 12), :] for i in range(6)]
@@ -638,26 +649,37 @@
         )
         for cg in range(4):
             b.wc_out[l, cg] = jnp.concatenate(pieces[cg], axis=0).astype(BF16)
-    for i, ref in enumerate((w_up, w_down)):
-        b.raw[0:288] = ref[...].astype(F32)
+    for i, ref in enumerate((b.w_up, b.w_down)):
+        b.raw[0:288] = read(ref)[...].astype(F32)
         for l in range(LAYERS):
             b.wm_out[l, FLAT * i : FLAT * (i + 1)] = b.raw[every(l, FLAT, 2), :].astype(BF16)
 
+    for zz in range(4):
+        for cc in range(2):
+            gg = 2 * (p % 2) + s // 4
+            row = pl.multiple_of(48 * (s % 4), 16)
+            send(
+                b.misc.at[0:48, :], b.gn_in.at[p // 2, pl.ds(row, 48), :],
+                dev(gg // 2, cc, zz, gg % 2), gn_sem, True,
+            )
     send_level(0)
+    send_level_qkv(1)
     send_level(1)
-    level_here(0)
+    level_qkv_here(0)
+    send_along("q", 0)
+    b.cotown_t[...] = read(b.cotangent)[...].T
     x_sem = [new_sems() for _ in range(LAYERS)]
     x_half = b.x_all.at[0, :, pl.ds(own, HALF)]
     arrived(x_half, tok_sem)
     send(x_half, x_half, sibling, x_sem[0])
+    relay("q", 0)
+    level_here(0)
     send_along("c", 0)
     send_along("m", 0)
-    relay_qkv(0)
     arrived(b.ln_in, len_sem)
     valid = b.ln_in[0:1, 0:1]
     key_at = lax.broadcasted_iota(jnp.int32, (FULL, 128), 0).astype(F32)
     b.bias[...] = jnp.where(key_at < valid, 0.0, -1e30)
-    arrived(b.gn_in, gn_sem)
 
     def gain_shift(l, k):
         columns = b.gn_in[k].astype(F32)
@@ -745,10 +767,17 @@
 
     def forward(l):
         x_own = b.x_all[l, :, pl.ds(own, HALF)]
-        arrived(b.wq_in.at[l, :, pl.ds(4 * (1 - c), 4)], relay_q[l])
+        relayed("q", l)
+        for n in range(24):
+            rows = slice(UNIT * n, UNIT * (n + 1))
+            start = QKV_AT + 2 * UNIT * (n % 3)
+            unit = b.w_in[l, n // 3 % 2, n // 6, start : start + 2 * UNIT].astype(F32)
+            b.left[rows] = unit[:UNIT]
+            b.right[rows] = unit[UNIT:]
         turned = []
         for cc in range(3):
-            nat = matrix_of(b.wq_in[l, cc])
+            rows = pl.ds(pl.multiple_of(PART * ((cc + g) % 3), UNIT), PART)
+            nat = jnp.concatenate([b.left[rows, :], b.right[rows, :][:, 0:64]], axis=1).astype(BF16)
             b.wn_q[l, cc] = nat
             turned.append(nat.T)
         b.q_t[l] = mm(turned[0], x_own).astype(BF16) * jnp.asarray(0.125, BF16)
@@ -763,6 +792,9 @@
         keys_values(own, x_own)
         arrived(b.x_all.at[l, :, pl.ds(other, HALF)], x_sem[l])
         keys_values(other, b.x_all[l, :, pl.ds(other, HALF)])
+
+        if l == 1:
+            send_cotangent()
 
         def one_head(h, carry):
             head = pl.multiple_of(HEAD * h, HEAD)
@@ -810,6 +842,8 @@
                 start = pl.multiple_of(PART * (2 * px + py) + HEAD * h, HEAD)
                 arrived(b.att_all.at[l, pl.ds(start, HEAD), :], att_sem[l][d] + h)
         relay("m", l)
+        if l == 0:
+            arrived(b.gn_in, gn_sem)
         branch = mm(columns_t, b.att_all[l])
         gain, shift = gain_shift(l, 0)
         finish = normalize_here(x_own.astype(F32) + branch, "1", l, gain, shift)
@@ -823,11 +857,11 @@
         down_t = nat.T
         middle = finish().astype(BF16)
         if l == 0:
-            send_qkv(1)
             level_here(1)
+            level_qkv_here(1)
+            send_along("q", 1)
             send_along("c", 1)
             send_along("m", 1)
-            send_cotangent()
         b.mid[l] = middle
 
         def one_block(i, carry):
@@ -852,22 +886,21 @@
     b.x_all[1, :, pl.ds(own, HALF)] = hidden.astype(BF16)
     x_half = b.x_all.at[1, :, pl.ds(own, HALF)]
     send(x_half, x_half, sibling, x_sem[1])
-    relay_qkv(1)
+    relay("q", 1)
     send_along("r", 1)
     send_along("r", 0)
     (hidden, one, two), grad = forward(1)
 
     mix_sem, tg_sem = new_sems(), new_sems()
 
-    def send_back(value, out_ref, in_ref, arrive):
-        out_ref[...] = value.astype(BF16)
+    def send_back(out_ref, in_ref, arrive):
         for k in range(4):
             send(
                 out_ref.at[:, ROWS * k : ROWS * (k + 1)], in_ref.at[pl.ds(g_rows, PART), :],
                 (seq_here, 4 * c + k), arrive, True,
             )
 
-    send_back(hidden, b.mix_out, b.mix_in, mix_sem)
+    b.mix_out[...] = hidden.astype(BF16)
 
     half_sem = {(name, l): new_sems() for l in range(LAYERS) for name in "moq"}
     level_sem = {(name, l): new_sems(3) for l in range(LAYERS) for name in "mo"}
@@ -894,11 +927,14 @@
         total = getattr(b, "gm_" + name)[l, z].astype(F32) + sum(four[l, i].astype(F32) for i in range(3))
         final = getattr(b, "gf_" + name)
         final[l] = total.astype(BF16)
-        send(final.at[l], getattr(b, "rg_" + name).at[l], dev(g // 2, g % 2, z, c), owner_sem[name, l], True)
+        return lambda: send(final.at[l], getattr(b, "rg_" + name).at[l], dev(g // 2, g % 2, z, c), owner_sem[name, l], True)
 
     def qkv_to_owners(l):
         arrived(b.sb_q.at[l], half_sem["q", l])
         b.gm_q[l] = (b.gb_q[l, pl.ds(4 * c, 4)].astype(F32) + b.sb_q[l].astype(F32)).astype(BF16)
+        return lambda: qkv_sends(l)
+
+    def qkv_sends(l):
         for k in range(4):
             for cc in range(3):
                 u = 32 * cc + 8 * g + 4 * c + k
@@ -949,8 +985,6 @@
         relay("r", l)
         second_grad = normalize_back_here(grad, "2", l, 1, known)
         b.sgb[l] = second_grad.astype(BF16)
-        if l + 1 < LAYERS:
-            qkv_to_owners(l + 1)
 
         def one_block(i, carry):
             rows = pl.ds(pl.multiple_of(FF_BLOCK * i, FF_BLOCK), FF_BLOCK)
@@ -979,8 +1013,10 @@
         flat_units(mm_nt(b.mid[l], b.eg[l]), b.gb_m.at[l], FLAT)
         to_sibling("m", l)
         if l + 1 < LAYERS:
-            to_owner("m", l + 1)
-            to_owner("o", l + 1)
+            later = [qkv_to_owners(l + 1), to_owner("m", l + 1), to_owner("o", l + 1)]
+        else:
+            later = [lambda: send_back(b.mix_out, b.mix_in, mix_sem)]
+        to_level("m", l)
         relayed("r", l)
         wide_rows(l, ROWS_AT, b.wn_r.at[l])
         for d, (fx, fy) in enumerate(((0, 1), (1, 0), (1, 1))):
@@ -992,8 +1028,9 @@
         flat_units(mm_nt(att, b.bg_all[l]), b.gb_o.at[l], 0)
         to_sibling("o", l)
         b.do_t[...] = mm(b.wn_r[l], b.bg_all[l]).astype(BF16)
-        to_level("m", l)
         to_level("o", l)
+        for sends in later:
+            sends()
 
         def one_head(h, carry):
             head = pl.multiple_of(HEAD * h, HEAD)
@@ -1027,10 +1064,11 @@
 
     grad = backward(1, grad, (one, two))
     grad = backward(0, grad)
-    send_back(grad, b.tg_out, b.tg_in, tg_sem)
-    qkv_to_owners(0)
-    to_owner("m", 0)
-    to_owner("o", 0)
+    b.tg_out[...] = grad.astype(BF16)
+    send_back(b.tg_out, b.tg_in, tg_sem)
+    qkv_to_owners(0)()
+    to_owner("m", 0)()
+    to_owner("o", 0)()
 
     arrived(b.mix_in, mix_sem)
     mixed[...] = b.mix_in[...].T
@@ -1099,6 +1137,7 @@
         raw(down_weight),
     )
     vmem = pl.BlockSpec(memory_space=pltpu.VMEM)
+    anywhere = pl.BlockSpec(memory_space=pl.ANY)
     shapes = (
         ((ROWS, D), BF16),
         ((ROWS, D), BF16),
@@ -1111,7 +1150,7 @@
     mixed, tokens_grad, g_qkv, g_out, g_up, g_down, g_norm = pl.pallas_call(
         fast_kernel,
         out_shape=tuple(jax.ShapeDtypeStruct(*shape) for shape in shapes),
-        in_specs=[vmem] * 2 + [pl.BlockSpec(memory_space=pltpu.SMEM)] + [vmem] * 6,
+        in_specs=[anywhere] * 2 + [pl.BlockSpec(memory_space=pltpu.SMEM)] + [anywhere] * 6,
         out_specs=tuple([vmem] * len(shapes)),
         scratch_shapes=[pltpu.SemaphoreType.DMA((SEMS,))] + [pltpu.VMEM(*entry) for entry in SCRATCH.values()],
         compiler_params=pltpu.CompilerParams(

time: 141 us -> 132 us (0.936)
  Pallas kernels: 139 us -> 130 us
    pallas_call x1, Pallas kernels: 137 us -> 128 us  [fast_device(): pl.pallas_call(fast_kernel, out_shape=tuple((jax.ShapeDtypeStruct(*shape)...]
where the time goes in v4:
time: 132 us
  Pallas kernels  130 us (98%)
  between operations  1.38 us (1%)
    pallas_call x1, Pallas kernels, fast_device(): pl.pallas_call(fast_kernel, out_shape=tuple((jax.ShapeDtypeStruct(*shape)...  128 us

profile of v4, /device:TPU:0, one launch (start us, length us, event | category | flops | bytes accessed | tf_op | source)
XLA Modules:
  0.0 131.8 jit_solution(3952458608470752076)
XLA Ops:
  1.3 128.2 %encoder.1 = (bf16[128,768]{1,0:T(8,128)(2,1)}, bf16[128,768]{1,0:T(8,128)(2,1)}, f32[2,13824]{1,0:T(2,128)}, f32[288,128]{1,0:T(8,128)}, f32[288,128]{1,0:T(8,1...) custom-call(bf16[128,768]{1,0:T(8,128)(2,1)} %bitcast.34, bf16[128,768]{1,0:T(8,128)(2,1)} %bitcast.35, s32[1]{0:T(128)S(6)} %copy.23.length, ...), custom_call_target="tpu_custom_call" | custom-call | tf_op jit(solution)/shard_map/encoder/pallas_call | solution.py:1150
  129.5 2.2 %hand_over.1 = (bf16[128,768]{1,0:T(8,128)(2,1)}, bf16[128,768]{1,0:T(8,128)(2,1)}, f32[2,13824]{1,0:T(2,128)}, f32[288,128]{1,0:T(8,128)}, f32[288,128]{1,0:T(8...) custom-call(bf16[128,768]{1,0:T(8,128)(2,1)} %get-tuple-element.23.refs_0_, ...), custom_call_target="tpu_custom_call" | custom-call | tf_op jit(solution)/shard_map/hand_over/pallas_call | solution.py:1164

commit v5 on v4

--- a/solution.py
+++ b/solution.py
@@ -317,7 +317,7 @@
 SHARD = QKV_AT + 3 * 2 * UNIT
 HEADS_HERE = HEADS // GROUPS
 KEY_BLOCK = 256
-FF_BLOCK = 128
+FF_BLOCK = 256
 SEMS = 512
 MESH = pl.DeviceIdType.MESH
 
@@ -467,7 +467,7 @@
 
 def fast_kernel(
     tokens_at, cotangent_at, length, gains_at, shifts_at, w_qkv_at, w_out_at, w_up_at, w_down_at,
-    mixed, tokens_grad, g_qkv, g_out, g_up, g_down, g_norm,
+    mixed, tokens_grad, g_qkv, g_out, g_up, g_down, g_gain, g_shift,
     sems, *scratch,
 ):
     b = types.SimpleNamespace(**dict(zip(SCRATCH, scratch)))
@@ -952,7 +952,7 @@
             lane_at == 2 * l + 1, shift_grad, 0.0
         )
 
-    def normalize_back_here(grad, name, l, k, known=None):
+    def normalize_back_here(grad, name, l, k, known=None, meanwhile=None):
         gain, _ = gain_shift(l, k)
         scaled = getattr(b, "xh" + name)[l]
         weighted = grad * gain
@@ -961,6 +961,8 @@
                 jnp.sum(weighted, axis=0, keepdims=True), jnp.sum(weighted * scaled, axis=0, keepdims=True)
             )
             norm_grads(grad, scaled, l, k)
+            if meanwhile is not None:
+                meanwhile()
             four = finish()
             one, two = (sum(f[i] for f in four) * (1.0 / D) for i in range(2))
         else:
@@ -994,7 +996,18 @@
 
         lax.fori_loop(0, PART_FF // FF_BLOCK, one_block, 0)
         middle_grad = second_grad + mm(b.wn_u[l], b.eg[l])
-        first_grad = normalize_back_here(middle_grad, "1", l, 0)
+
+        def weight_grads():
+            grads = mm_nt(b.act[l], b.sgb[l])
+            b.left[...] = grads[:, :128]
+            b.right[:, 0:64] = grads[:, 128:]
+            for i, part in enumerate(triples_from_rows(PART_FF // 2, b.left, b.right)):
+                b.raw[every(i, PART_FF // 2, 3), :] = part
+            scatter_raw(b.gb_m.at[l], 0)
+            flat_units(mm_nt(b.mid[l], b.eg[l]), b.gb_m.at[l], FLAT)
+            to_sibling("m", l)
+
+        first_grad = normalize_back_here(middle_grad, "1", l, 0, None, weight_grads)
         b.fg[...] = first_grad
         b.bg_all[l, pl.ds(g_rows, PART), :] = first_grad.astype(BF16)
         piece = b.bg_all.at[l, pl.ds(g_rows, PART), :]
@@ -1004,14 +1017,6 @@
             norm_grads(grad, b.xh2[l], l, 1)
         if l == 0:
             send_norm_grads()
-        grads = mm_nt(b.act[l], b.sgb[l])
-        b.left[...] = grads[:, :128]
-        b.right[:, 0:64] = grads[:, 128:]
-        for i, part in enumerate(triples_from_rows(PART_FF // 2, b.left, b.right)):
-            b.raw[every(i, PART_FF // 2, 3), :] = part
-        scatter_raw(b.gb_m.at[l], 0)
-        flat_units(mm_nt(b.mid[l], b.eg[l]), b.gb_m.at[l], FLAT)
-        to_sibling("m", l)
         if l + 1 < LAYERS:
             later = [qkv_to_owners(l + 1), to_owner("m", l + 1), to_owner("o", l + 1)]
         else:
@@ -1059,6 +1064,8 @@
         to_sibling("q", l)
         here = mm(w_q, b.dq_t[...])
         here += mm(w_k, b.dk_t[:, pl.ds(own, HALF)]) + mm(w_v, b.dv_t[:, pl.ds(own, HALF)])
+        if l == 0:
+            qkv_to_owners(0)()
         arrived(b.dx_in.at[l], dx_sem[l])
         return b.fg[...] + here + b.dx_in[l]
 
@@ -1066,7 +1073,6 @@
     grad = backward(0, grad)
     b.tg_out[...] = grad.astype(BF16)
     send_back(b.tg_out, b.tg_in, tg_sem)
-    qkv_to_owners(0)()
     to_owner("m", 0)()
     to_owner("o", 0)()
 
@@ -1087,7 +1093,10 @@
     arrived(b.tg_in, tg_sem)
     tokens_grad[...] = b.tg_in[...].T
     arrived(b.gs_in, gs_sem)
-    g_norm[...] = sum(b.gs_in[i] for i in range(8))
+    norms = sum(b.gs_in[i] for i in range(8))
+    for k, out in enumerate((g_gain, g_shift)):
+        for l in range(LAYERS):
+            out[l : l + 1, :] = norms[2 * l + k : 2 * l + k + 1, 0 : PART // 4]
 
     for k in range(108):
         g_qkv[:, 128 * k : 128 * (k + 1)] = b.raw[2 * k : 2 * k + 2]
@@ -1108,12 +1117,8 @@
 
 
 def hand_over(*refs):
-    plain, norms, outs = refs[:6], refs[6], refs[7:]
-    for ref, out in zip(plain, outs):
+    for ref, out in zip(refs[:8], refs[8:]):
         out[...] = ref[...]
-    for k in range(2):
-        for l in range(LAYERS):
-            outs[6 + k][l : l + 1, :] = norms[2 * l + k : 2 * l + k + 1, 0 : PART // 4]
 
 
 def fast_device(
@@ -1145,9 +1150,10 @@
         ((LAYERS * FLAT, 128), F32),
         ((LAYERS * FLAT, 128), F32),
         ((LAYERS * FLAT, 128), F32),
-        ((8, 128), F32),
+        ((LAYERS, PART // 4), F32),
+        ((LAYERS, PART // 4), F32),
     )
-    mixed, tokens_grad, g_qkv, g_out, g_up, g_down, g_norm = pl.pallas_call(
+    results = pl.pallas_call(
         fast_kernel,
         out_shape=tuple(jax.ShapeDtypeStruct(*shape) for shape in shapes),
         in_specs=[anywhere] * 2 + [pl.BlockSpec(memory_space=pltpu.SMEM)] + [anywhere] * 6,
@@ -1158,16 +1164,13 @@
         ),
         name="encoder",
     )(*operands)
-    results = (mixed, tokens_grad, g_qkv, g_out, g_up, g_down)
-    shapes = [jax.ShapeDtypeStruct(array.shape, array.dtype) for array in results]
-    shapes += [jax.ShapeDtypeStruct((LAYERS, PART // 4), F32)] * 2
     mixed, tokens_grad, g_qkv, g_out, g_up, g_down, g_gain, g_shift = pl.pallas_call(
         hand_over,
-        out_shape=tuple(shapes),
-        in_specs=[vmem] * (len(results) + 1),
+        out_shape=tuple(jax.ShapeDtypeStruct(*shape) for shape in shapes),
+        in_specs=[vmem] * len(shapes),
         out_specs=tuple([vmem] * len(shapes)),
         name="hand_over",
-    )(*results, g_norm)
+    )(*results)
     return (
         mixed[None],
         tokens_grad[None],

time: 132 us -> 129 us (0.977); the launches traced: 132 us -> 127 us
  Pallas kernels: 130 us -> 126 us
    pallas_call x1, Pallas kernels: 128 us -> 123 us  [fast_device(): pl.pallas_call(fast_kernel, out_shape=tuple((jax.ShapeDtypeStruct(*shape)...]
where the time goes in v5:
time: 129 us; the launch traced here: 127 us
  Pallas kernels  126 us (98%)
  between operations  1.4 us (1%)
    pallas_call x1, Pallas kernels, fast_device(): pl.pallas_call(fast_kernel, out_shape=tuple((jax.ShapeDtypeStruct(*shape)...  123 us

profile of v5, /device:TPU:0, one launch (start us, length us, event | category | flops | bytes accessed | tf_op | source)
XLA Modules:
  0.0 127.1 jit_solution(12939187024368281040)
XLA Ops:
  1.3 123.5 %encoder.1 = (bf16[128,768]{1,0:T(8,128)(2,1)}, bf16[128,768]{1,0:T(8,128)(2,1)}, f32[2,13824]{1,0:T(2,128)}, f32[288,128]{1,0:T(8,128)}, f32[288,128]{1,0:T(8,1...) custom-call(bf16[128,768]{1,0:T(8,128)(2,1)} %bitcast.34, bf16[128,768]{1,0:T(8,128)(2,1)} %bitcast.35, ...), custom_call_target="tpu_custom_call" | custom-call | tf_op jit(solution)/shard_map/encoder/pallas_call | solution.py:1156
  124.8 2.2 %hand_over.1 = (bf16[128,768]{1,0:T(8,128)(2,1)}, bf16[128,768]{1,0:T(8,128)(2,1)}, f32[2,13824]{1,0:T(2,128)}, f32[288,128]{1,0:T(8,128)}, f32[288,128]{1,0:T(8...) custom-call(bf16[128,768]{1,0:T(8,128)(2,1)} %get-tuple-element.24.refs_0_, ...), custom_call_target="tpu_custom_call" | custom-call | tf_op jit(solution)/shard_map/hand_over/pallas_call | solution.py:1167
